TPU v7x, 128 devices: a whole 4x4x4 slice. The times are simulated.
128 devices in a mesh: lat: 4 (over y), lon: 32 (over x, z, core).
Axes of the slice: x: 4, y: 4, z: 4, core: 2. Of those that a mesh axis runs over, the one named last changes fastest.
Arguments:
- conc: bfloat16 [128, 64, 8192], P('lat', None, 'lon'), may hold values from -6 to 6
- dep_owner: int32 [32, 128, 4], P('lon', 'lat'), may hold values from 0 to 14, all different within a row; in each aligned block of 32 rows (0 to 31, 32 to 63, ..., all dimensions but the last counted through in order) at most 17 rows name the same one
- dep_row: int32 [32, 128, 4], P('lon', 'lat'), may hold values from 0 to 31
- dep_weight: float32 [32, 128, 4], P('lon', 'lat'), may hold values from 0.05 to 0.5
- dep_count: int32 [32, 128], P('lon', 'lat'), may hold values from 1 to 4
- zonal_offset: int32 [128], P('lat'), may hold values from -2 to 2
- agg_rates: float32 [4, 128, 8192], P(None, 'lat', 'lon'), may hold values from 0.1 to 1
- toeplitz: bfloat16 [4, 127], replicated, may hold values from -0.75 to 0.75
- settle: float32 [64], replicated, may hold values from 0.05 to 0.5
- kappa: float32 [128, 8192], P('lat', 'lon'), may hold values from 0.02 to 0.2
Outputs:
- updated: float32 [128, 64, 8192], P('lat', None, 'lon')
Inputs may be any that keep to these rules, and one draw needn't show every extreme that they name: `dep_owner`: the 4 entries of a row name different neighbour blocks; among the rows of one device no neighbour block is named by more than 17 entries, and in some device's rows one is named exactly 17 times; every value is named somewhere. `dep_count`: entries of a row at or past its count are padding.
All inputs are finite; a program needn't handle non-finite values.
Results may differ from a plain program's by a relative error of at most 0.00092.
Values may be sent and summed in bfloat16 or wider, within the bound.
A program may use at most 64 MiB of HBM per device.

v0:
```python
import jax
import jax.numpy as jnp
from jax import lax
from jax.sharding import PartitionSpec as P


def from_behind(value, axis, steps):
    count = lax.axis_size(axis)
    pairs = [(source, (source + steps) % count) for source in range(count)]
    return lax.ppermute(value, axis, pairs)


def from_behind_2(value, axis, steps):
    count = lax.axis_size(axis)
    initial, last = (max(0, -steps), min(count, count - steps))
    return lax.ppermute(value, axis, [(source, source + steps) for source in range(initial, last)])


def with_halo(value, sides, width, wrap):
    for axis, dim in sides:
        size, length = (lax.axis_size(axis), value.shape[dim])
        up = [(i, (i + 1) % size) for i in range(size if wrap else size - 1)]
        down = [(j, i) for i, j in up]
        last = lax.slice_in_dim(value, length - width, length, axis=dim)
        initial = lax.slice_in_dim(value, 0, width, axis=dim)
        before = lax.ppermute(last, axis, up)
        after = lax.ppermute(initial, axis, down)
        value = jnp.concatenate([before, value, after], axis=dim)
    return value


def toeplitz_stack(toeplitz, bins):
    flipped = toeplitz[:, ::-1]
    return jnp.stack([flipped[:, bins - 1 - i : 2 * bins - 1 - i] for i in range(bins)], axis=1)


def shift_rows(widened, displace, start, length):
    result = jnp.zeros(widened.shape[:2] + (length,), widened.dtype)
    for step in range(-2, 3):
        window = widened[:, :, start - step : start - step + length]
        result = result + jnp.where(displace == step, window, jnp.zeros_like(window))
    return result


def request_along_lon(values, amount):
    if amount == 0:
        return values
    return from_behind(values, "lon", amount)


def request_along_lat(values, amount):
    if amount == 0:
        return values
    return from_behind_2(values, "lat", amount)


def single_along_lon(values, amount):
    if amount == 0:
        return values
    return from_behind(values, "lon", amount)


def single_along_lat(values, amount):
    if amount == 0:
        return values
    return from_behind_2(values, "lat", amount)


def body(
    conc,
    dep_owner,
    dep_row,
    dep_weight,
    dep_count,
    zonal_offset,
    agg_rates,
    toeplitz,
    settle,
    kappa,
):
    rows_dev, bins, width = conc.shape
    entries = dep_owner.shape[2]
    blocks_near = 15
    capacity = max(2, 2 * rows_dev * entries // blocks_near)
    owners = dep_owner.reshape(-1)
    sources = dep_row.reshape(-1)
    owner_hot = (owners[:, None] == jnp.arange(blocks_near, dtype=jnp.int32)[None, :]).astype(
        jnp.int32
    )
    earlier = jnp.cumsum(owner_hot, axis=0) - owner_hot
    slots = jnp.sum(earlier * owner_hot, axis=1)
    slot_hot = (slots[:, None] == jnp.arange(capacity, dtype=jnp.int32)[None, :]).astype(jnp.int32)
    requests = jnp.einsum("ed,ec->dc", owner_hot * sources[:, None], slot_hot).reshape(
        3, 5, capacity
    )
    moved = jnp.stack([request_along_lon(requests[:, c], c - 2) for c in range(5)], axis=1)
    wanted = jnp.stack([request_along_lat(moved[a], a - 1) for a in range(3)], axis=0)
    outgoing = jnp.take(conc, wanted.reshape(-1), axis=0).reshape(3, 5, capacity, bins, width)
    matrices = toeplitz_stack(toeplitz, bins)
    growth = jnp.zeros((rows_dev, bins, width), jnp.float32)
    for q in range(matrices.shape[0]):
        product = jnp.einsum("ij,rjx->rix", matrices[q], conc, preferred_element_type=jnp.float32)
        growth = growth + agg_rates[q][:, None, :] * product
    pieces = []
    for a in range(3):
        for c in range(5):
            piece = single_along_lon(outgoing[a, c], 2 - c)
            pieces.append(single_along_lat(piece, 1 - a))
    arrived = jnp.stack(pieces, axis=0)
    arrived = arrived.reshape(blocks_near * capacity, bins, width)
    positions = (owners * capacity + slots).reshape(rows_dev, entries)
    live_weight = jnp.where(
        jnp.arange(entries, dtype=jnp.int32)[None, :] < dep_count[0][:, None],
        dep_weight[0],
        jnp.float32(0.0),
    )
    summed = jnp.zeros((rows_dev, bins, width), jnp.float32)
    for k in range(entries):
        summed = summed + live_weight[:, k, None, None] * jnp.take(
            arrived, positions[:, k], axis=0
        ).astype(jnp.float32)
    remapped = summed.astype(jnp.bfloat16)
    displace = zonal_offset[:, None, None]
    widened = with_halo(remapped, (("lon", 2),), 2, True)
    shifted = shift_rows(widened, displace, 2, width)
    sided = with_halo(shifted, (("lon", 2),), 1, True)
    east_cells = sided[:, :, 2:].astype(jnp.float32)
    west_cells = sided[:, :, :-2].astype(jnp.float32)
    stacked = with_halo(shifted, (("lat", 0),), 1, False).astype(jnp.float32)
    center = shifted.astype(jnp.float32)
    neighbours = stacked[2:] + stacked[:-2] + east_cells + west_cells
    diffusion = kappa[:, None, :] * (neighbours - 4.0 * center)
    return center + diffusion + growth - settle[None, :, None] * conc.astype(jnp.float32)


def solution(mesh):
    return jax.shard_map(
        body,
        mesh=mesh,
        in_specs=(
            P("lat", None, "lon"),
            P("lon", "lat", None),
            P("lon", "lat", None),
            P("lon", "lat", None),
            P("lon", "lat"),
            P("lat"),
            P(None, "lat", "lon"),
            P(),
            P(),
            P("lat", "lon"),
        ),
        out_specs=P("lat", None, "lon"),
        check_vma=False,
    )
```

profile of v0, /device:TPU:0, one launch (start us, length us, event | category | flops | bytes accessed | tf_op | source)
XLA Modules:
  0.0 263.7 jit_solution(3375684760601165412)
XLA Ops:
  2.6 6.4 %collective-permute-start = (s32[3,17]{1,0:T(4,128)S(1)}, s32[3,17]{1,0:T(4,128)S(1)}, u32[]{:S(2)}, u32[]{:S(2)}) collective-permute-start(s32[3,17]{1,0:T(4,128)S(1)} %bitcast.276), channel_id=1, source_target_pairs={{0,30},{1,31},{2,0},{3,1},{4,2},{5,3},{6,4},{7,5},{8,6},{9,7},{10,... | collective-permute-start | bytes 620 | tf_op jit(solution)/shard_map/ppermute | solution.py:10
  10.2 1.5 fusion.35
  11.7 1.5 fusion.34
  13.1 1.5 fusion.33
  23.2 1.7 fusion.26
  25.2 1.3 collective-permute-start.4
  26.5 4.5 %collective-permute-start.5 = (s32[5,17]{1,0:T(8,128)S(1)}, s32[5,17]{1,0:T(8,128)S(1)}, u32[]{:S(2)}, u32[]{:S(2)}) collective-permute-start(s32[5,17]{1,0:T(8,128)S(1)} %get-tuple-element.39), channel_id=1, source_target_pairs={{0,32},{32,64},{64,96},{1,33},{33,65},{65,97},{2,34},{34,66},{66,9... | collective-permute-start | bytes 1028 | tf_op jit(solution)/shard_map/ppermute | solution.py:16
  32.5 8.5 %gather_fusion = bf16[255,64,256]{2,1,0:T(8,128)(2,1)} fusion(bf16[32,64,256]{2,1,0:T(8,128)(2,1)S(1)} %copy-done, s32[1024]{0:T(1024)S(1)} %pad_clamp_fusion.4), kind=kCustom, calls=%fused_computation.4 | custom fusion | bytes 16712700 | tf_op jit(solution)/shard_map/jit(_take)/gather | solution.py:98
  41.0 7.5 %broadcast_select_fusion = bf16[3,5,17,64,256]{4,3,2,1,0:T(8,128)(2,1)} fusion(bf16[3,5,17,64,256]{4,3,2,1,0:T(8,128)(2,1)} %bitcast.206, pred[3,5,17]{2,1,0:T(8,128)(4,1)S(1)} %compare_and_fusion), kind=kLoop, calls=%fused_computation.5 | loop fusion | flops 4177920 | bytes 16711935 | tf_op jit(solution)/shard_map/jit(_take)/select_n | solution.py:98
  48.4 3.9 %slice_bitcast_fusion = (bf16[17,64,256]{2,1,0:T(8,128)(2,1)S(1)}, bf16[17,64,256]{2,1,0:T(8,128)(2,1)S(1)}, bf16[17,64,256]{2,1,0:T(8,128)(2,1)S(1)}, bf16[17,6...) fusion(bf16[3,5,17,64,256]{4,3,2,1,0:T(8,128)(2,1)} %broadcast_, ...), kind=kLoop, calls=%fused_computation.35 | loop fusion | bytes 15597568 | tf_op jit(solution)/shard_map/squeeze | solution.py:107
  52.6 1.8 fusion.27
  54.3 5.1 %collective-permute-start.11 = (bf16[17,64,256]{2,1,0:T(8,128)(2,1)S(1)}, bf16[17,64,256]{2,1,0:T(8,128)(2,1)S(1)}, u32[]{:S(2)}, u32[]{:S(2)}) collective-permute-start(bf16[17,64,256]{2,1,0:T(8,128)(2,1)S(1)} %get-tuple-element.24), channel_id=1, source_target_pairs={{0,31},{1,0},{2,1},{3,2},{4,3},{5,4},{6,5},{7,6},{8,7},{9,8},{10,9... | collective-permute-start | bytes 1671176 | tf_op jit(solution)/shard_map/ppermute | solution.py:10
  59.4 11.9 %collective-permute-done.6 = bf16[17,64,256]{2,1,0:T(8,128)(2,1)S(1)} collective-permute-done((bf16[17,64,256]{2,1,0:T(8,128)(2,1)S(1)}, bf16[17,64,256]{2,1,0:T(8,128)(2,1)S(1)}, u32[]{:S(2)}, u32[]{:S(2)}) %collective-permute-start.6) | collective-permute-done | bytes 557088 | tf_op jit(solution)/shard_map/ppermute | solution.py:10
  71.3 4.3 %collective-permute-start.7 = (bf16[17,64,256]{2,1,0:T(8,128)(2,1)S(1)}, bf16[17,64,256]{2,1,0:T(8,128)(2,1)S(1)}, u32[]{:S(2)}, u32[]{:S(2)}) collective-permute-start(bf16[17,64,256]{2,1,0:T(8,128)(2,1)S(1)} %collective-permute-done.6), channel_id=1, source_target_pairs={{0,32},{32,64},{64,96},{1,33},{33,65},{65,97},{2,34},{34,66},{66,9... | collective-permute-start | bytes 1671176 | tf_op jit(solution)/shard_map/ppermute | solution.py:16
  75.7 1.4 collective-permute-start.13
  77.1 3.5 %collective-permute-start.9 = (bf16[17,64,256]{2,1,0:T(8,128)(2,1)S(1)}, bf16[17,64,256]{2,1,0:T(8,128)(2,1)S(1)}, u32[]{:S(2)}, u32[]{:S(2)}) collective-permute-start(bf16[17,64,256]{2,1,0:T(8,128)(2,1)S(1)} %collective-permute-done.8), channel_id=1, source_target_pairs={{0,32},{32,64},{64,96},{1,33},{33,65},{65,97},{2,34},{34,66},{66,9... | collective-permute-start | bytes 1671176 | tf_op jit(solution)/shard_map/ppermute | solution.py:16
  80.5 3.4 %collective-permute-start.10 = (bf16[17,64,256]{2,1,0:T(8,128)(2,1)S(1)}, bf16[17,64,256]{2,1,0:T(8,128)(2,1)S(1)}, u32[]{:S(2)}, u32[]{:S(2)}) collective-permute-start(bf16[17,64,256]{2,1,0:T(8,128)(2,1)S(1)} %get-tuple-element.25), channel_id=1, source_target_pairs={{0,32},{32,64},{64,96},{1,33},{33,65},{65,97},{2,34},{34,66},{66,9... | collective-permute-start | bytes 1671176 | tf_op jit(solution)/shard_map/ppermute | solution.py:16
  84.8 3.9 %collective-permute-done.7 = bf16[17,64,256]{2,1,0:T(8,128)(2,1)S(1)} collective-permute-done((bf16[17,64,256]{2,1,0:T(8,128)(2,1)S(1)}, bf16[17,64,256]{2,1,0:T(8,128)(2,1)S(1)}, u32[]{:S(2)}, u32[]{:S(2)}) %collective-permute-start.7) | collective-permute-done | bytes 557088 | tf_op jit(solution)/shard_map/ppermute | solution.py:16
  88.7 4.4 %collective-permute-start.12 = (bf16[17,64,256]{2,1,0:T(8,128)(2,1)S(1)}, bf16[17,64,256]{2,1,0:T(8,128)(2,1)S(1)}, u32[]{:S(2)}, u32[]{:S(2)}) collective-permute-start(bf16[17,64,256]{2,1,0:T(8,128)(2,1)S(1)} %collective-permute-done.11), channel_id=1, source_target_pairs={{0,32},{32,64},{64,96},{1,33},{33,65},{65,97},{2,34},{34,66},{66,9... | collective-permute-start | bytes 1671176 | tf_op jit(solution)/shard_map/ppermute | solution.py:16
  94.0 6.6 %collective-permute-done.9 = bf16[17,64,256]{2,1,0:T(8,128)(2,1)S(1)} collective-permute-done((bf16[17,64,256]{2,1,0:T(8,128)(2,1)S(1)}, bf16[17,64,256]{2,1,0:T(8,128)(2,1)S(1)}, u32[]{:S(2)}, u32[]{:S(2)}) %collective-permute-start.9) | collective-permute-done | bytes 557088 | tf_op jit(solution)/shard_map/ppermute | solution.py:16
  100.6 4.4 %collective-permute-start.14 = (bf16[17,64,256]{2,1,0:T(8,128)(2,1)S(1)}, bf16[17,64,256]{2,1,0:T(8,128)(2,1)S(1)}, u32[]{:S(2)}, u32[]{:S(2)}) collective-permute-start(bf16[17,64,256]{2,1,0:T(8,128)(2,1)S(1)} %collective-permute-done.13), channel_id=1, source_target_pairs={{0,32},{32,64},{64,96},{1,33},{33,65},{65,97},{2,34},{34,66},{66,9... | collective-permute-start | bytes 1671176 | tf_op jit(solution)/shard_map/ppermute | solution.py:16
  105.9 6.7 %collective-permute-done.10 = bf16[17,64,256]{2,1,0:T(8,128)(2,1)S(1)} collective-permute-done((bf16[17,64,256]{2,1,0:T(8,128)(2,1)S(1)}, bf16[17,64,256]{2,1,0:T(8,128)(2,1)S(1)}, u32[]{:S(2)}, u32[]{:S(2)}) %collective-permute-start.10) | collective-permute-done | bytes 557088 | tf_op jit(solution)/shard_map/ppermute | solution.py:16
  113.4 11.0 %collective-permute-done.12 = bf16[17,64,256]{2,1,0:T(8,128)(2,1)S(1)} collective-permute-done((bf16[17,64,256]{2,1,0:T(8,128)(2,1)S(1)}, bf16[17,64,256]{2,1,0:T(8,128)(2,1)S(1)}, u32[]{:S(2)}, u32[]{:S(2)}) %collective-permute-start.12) | collective-permute-done | bytes 557088 | tf_op jit(solution)/shard_map/ppermute | solution.py:16
  124.5 1.3 collective-permute-start.18
  126.7 4.0 %collective-permute-done.14 = bf16[17,64,256]{2,1,0:T(8,128)(2,1)S(1)} collective-permute-done((bf16[17,64,256]{2,1,0:T(8,128)(2,1)S(1)}, bf16[17,64,256]{2,1,0:T(8,128)(2,1)S(1)}, u32[]{:S(2)}, u32[]{:S(2)}) %collective-permute-start.14) | collective-permute-done | bytes 557088 | tf_op jit(solution)/shard_map/ppermute | solution.py:16
  132.4 5.1 %collective-permute-start.24 = (bf16[17,64,256]{2,1,0:T(8,128)(2,1)S(1)}, bf16[17,64,256]{2,1,0:T(8,128)(2,1)S(1)}, u32[]{:S(2)}, u32[]{:S(2)}) collective-permute-start(bf16[17,64,256]{2,1,0:T(8,128)(2,1)S(1)} %get-tuple-element.15), channel_id=1, source_target_pairs={{0,31},{1,0},{2,1},{3,2},{4,3},{5,4},{6,5},{7,6},{8,7},{9,8},{10,9... | collective-permute-start | bytes 1671176 | tf_op jit(solution)/shard_map/ppermute | solution.py:10
  137.5 2.0 collective-permute-start.26
  140.4 8.8 %collective-permute-done.19 = bf16[17,64,256]{2,1,0:T(8,128)(2,1)S(1)} collective-permute-done((bf16[17,64,256]{2,1,0:T(8,128)(2,1)S(1)}, bf16[17,64,256]{2,1,0:T(8,128)(2,1)S(1)}, u32[]{:S(2)}, u32[]{:S(2)}) %collective-permute-start.19) | collective-permute-done | bytes 557088 | tf_op jit(solution)/shard_map/ppermute | solution.py:10
  150.5 1.9 fusion.16
  157.2 1.3 collective-permute-start.27
  159.3 7.8 %collective-permute-done.20 = bf16[17,64,256]{2,1,0:T(8,128)(2,1)S(1)} collective-permute-done((bf16[17,64,256]{2,1,0:T(8,128)(2,1)S(1)}, bf16[17,64,256]{2,1,0:T(8,128)(2,1)S(1)}, u32[]{:S(2)}, u32[]{:S(2)}) %collective-permute-start.20) | collective-permute-done | bytes 557088 | tf_op jit(solution)/shard_map/ppermute | solution.py:16
  168.0 11.1 %collective-permute-done.22 = bf16[17,64,256]{2,1,0:T(8,128)(2,1)S(1)} collective-permute-done((bf16[17,64,256]{2,1,0:T(8,128)(2,1)S(1)}, bf16[17,64,256]{2,1,0:T(8,128)(2,1)S(1)}, u32[]{:S(2)}, u32[]{:S(2)}) %collective-permute-start.22) | collective-permute-done | bytes 557088 | tf_op jit(solution)/shard_map/ppermute | solution.py:16
  179.9 11.1 %collective-permute-done.23 = bf16[17,64,256]{2,1,0:T(8,128)(2,1)S(1)} collective-permute-done((bf16[17,64,256]{2,1,0:T(8,128)(2,1)S(1)}, bf16[17,64,256]{2,1,0:T(8,128)(2,1)S(1)}, u32[]{:S(2)}, u32[]{:S(2)}) %collective-permute-start.23) | collective-permute-done | bytes 557088 | tf_op jit(solution)/shard_map/ppermute | solution.py:16
  191.9 6.0 %collective-permute-done.25 = bf16[17,64,256]{2,1,0:T(8,128)(2,1)S(1)} collective-permute-done((bf16[17,64,256]{2,1,0:T(8,128)(2,1)S(1)}, bf16[17,64,256]{2,1,0:T(8,128)(2,1)S(1)}, u32[]{:S(2)}, u32[]{:S(2)}) %collective-permute-start.25) | collective-permute-done | bytes 557088 | tf_op jit(solution)/shard_map/ppermute | solution.py:16
  198.7 5.1 %collective-permute-done.27 = bf16[17,64,256]{2,1,0:T(8,128)(2,1)S(1)} collective-permute-done((bf16[17,64,256]{2,1,0:T(8,128)(2,1)S(1)}, bf16[17,64,256]{2,1,0:T(8,128)(2,1)S(1)}, u32[]{:S(2)}, u32[]{:S(2)}) %collective-permute-start.27) | collective-permute-done | bytes 557088 | tf_op jit(solution)/shard_map/ppermute | solution.py:16
  204.7 5.0 %gather_fusion.1 = bf16[32,64,256]{2,1,0:T(8,128)(2,1)} fusion(bf16[255,64,256]{2,1,0:T(8,128)(2,1)} %bitcast.44, s32[1024]{0:T(1024)S(1)} %get-tuple-element.128), kind=kCustom, calls=%fused_computation.clone | custom fusion | bytes 2097280 | tf_op jit(solution)/shard_map/jit(_take)/gather | solution.py:119
  209.6 4.9 %gather_fusion.2 = bf16[32,64,256]{2,1,0:T(8,128)(2,1)} fusion(bf16[255,64,256]{2,1,0:T(8,128)(2,1)} %bitcast.44, s32[1024]{0:T(1024)S(1)} %get-tuple-element.127), kind=kCustom, calls=%fused_computation.1.clone | custom fusion | bytes 2097280 | tf_op jit(solution)/shard_map/jit(_take)/gather | solution.py:119
  214.6 5.0 %gather_fusion.3 = bf16[32,64,256]{2,1,0:T(8,128)(2,1)} fusion(bf16[255,64,256]{2,1,0:T(8,128)(2,1)} %bitcast.44, s32[1024]{0:T(1024)S(1)} %get-tuple-element.126), kind=kCustom, calls=%fused_computation.2.clone | custom fusion | bytes 2097280 | tf_op jit(solution)/shard_map/jit(_take)/gather | solution.py:119
  219.5 5.0 %gather_fusion.4 = bf16[32,64,256]{2,1,0:T(8,128)(2,1)} fusion(bf16[255,64,256]{2,1,0:T(8,128)(2,1)} %bitcast.44, s32[1024]{0:T(1024)S(1)} %get-tuple-element.125), kind=kCustom, calls=%fused_computation.3.clone | custom fusion | bytes 2097280 | tf_op jit(solution)/shard_map/jit(_take)/gather | solution.py:119
  224.5 2.9 %add_convert_fusion = bf16[32,64,256]{2,1,0:T(8,128)(2,1)S(1)} fusion(bf16[32,64,256]{2,1,0:T(8,128)(2,1)} %gather_fusion.4, bf16[32,64,256]{2,1,0:T(8,128)(2,1)} %gather_fusion.3, bf16[32,64,256]{2,1,0:T(8,128)(2,1)} %gather_fusion.2, bf16[32,64,256]{2,1,0:T(8,128)(2,1)} %gather_fusion.1, f32[32]{0:T(128)S(1)} %get-tuple-element.47, ...), kind=kLoop, calls=%fused_computation.15 | loop fusion | flops 8388608 | bytes 5243520 | tf_op jit(solution)/shard_map/convert_element_type | solution.py:122
  228.3 6.2 %collective-permute-done.28 = bf16[32,64,2]{2,1,0:T(8,128)(2,1)S(1)} collective-permute-done((bf16[32,64,2]{2,1,0:T(8,128)(2,1)S(1)}, bf16[32,64,2]{2,1,0:T(8,128)(2,1)S(1)}, u32[]{:S(2)}, u32[]{:S(2)}) %collective-permute-start.28) | collective-permute-done | bytes 8224 | tf_op jit(solution)/shard_map/ppermute | solution.py:27
  234.5 5.3 %collective-permute-done.29 = bf16[32,64,2]{2,1,0:T(8,128)(2,1)S(1)} collective-permute-done((bf16[32,64,2]{2,1,0:T(8,128)(2,1)S(1)}, bf16[32,64,2]{2,1,0:T(8,128)(2,1)S(1)}, u32[]{:S(2)}, u32[]{:S(2)}) %collective-permute-start.29) | collective-permute-done | bytes 8224 | tf_op jit(solution)/shard_map/ppermute | solution.py:26
  239.8 3.1 %fusion.9 = bf16[32,64,256]{2,1,0:T(8,128)(2,1)S(1)} fusion(bf16[32,64,2]{2,1,0:T(8,128)(2,1)S(1)} %collective-permute-done.29, bf16[32,64,256]{2,1,0:T(8,128)(2,1)S(1)} %add_convert_fusion, bf16[32,64,2]{2,1,0:T(8,128)(2,1)S(1)} %collective-permute-done.28, pred[32]{0:T(512)(128)(4,1)S(1)} %get-tuple-element.123, pred[32]{0:T(512)(128)(4,1)S(1)} %get-tuple-element.124, ...), kind=kLoop, calls=%fused_computation.24 | loop fusion | flops 16252928 | bytes 2113696 | tf_op jit(solution)/shard_map/add | solution.py:41
  242.9 3.6 %collective-permute-start.30 = (bf16[1,64,256]{2,1,0:T(8,128)(2,1)S(1)}, bf16[1,64,256]{2,1,0:T(8,128)(2,1)S(1)}, u32[]{:S(2)}, u32[]{:S(2)}) collective-permute-start(bf16[1,64,256]{2,1,0:T(8,128)(2,1)S(1)} %get-tuple-element.30), channel_id=1, source_target_pairs={{0,32},{32,64},{64,96},{1,33},{33,65},{65,97},{2,34},{34,66},{66,9... | collective-permute-start | bytes 98312 | tf_op jit(solution)/shard_map/ppermute | solution.py:26
  248.8 3.6 %collective-permute-done.31 = bf16[1,64,256]{2,1,0:T(8,128)(2,1)S(1)} collective-permute-done((bf16[1,64,256]{2,1,0:T(8,128)(2,1)S(1)}, bf16[1,64,256]{2,1,0:T(8,128)(2,1)S(1)}, u32[]{:S(2)}, u32[]{:S(2)}) %collective-permute-start.31) | collective-permute-done | bytes 32800 | tf_op jit(solution)/shard_map/ppermute | solution.py:27
  252.6 2.4 collective-permute-done.32
  255.0 5.3 %collective-permute-done.33 = bf16[32,64,1]{2,1,0:T(8,128)(2,1)S(1)} collective-permute-done((bf16[32,64,1]{2,1,0:T(8,128)(2,1)S(1)}, bf16[32,64,1]{2,1,0:T(8,128)(2,1)S(1)}, u32[]{:S(2)}, u32[]{:S(2)}) %collective-permute-start.33) | collective-permute-done | bytes 4128 | tf_op jit(solution)/shard_map/ppermute | solution.py:26
  260.3 3.4 %fusion.3 = f32[32,64,256]{2,1,0:T(8,128)} fusion(bf16[32,64,256]{2,1,0:T(8,128)(2,1)S(1)} %fusion.9, f32[34,64,256]{2,1,0:T(8,128)S(1)} %maximum_convert_fusion, bf16[32,64,256]{2,1,0:T(8,128)(2,1)S(1)} %copy-done, f32[64,32,256]{2,0,1:T(8,128)S(1)} %fusion.25, f32[64,32,256]{2,0,1:T(8,128)S(1)} %copy-done.1, f32[64,32,256]{2,0,1:T(8,128)S(1)} %copy-done.2, ...), kind=kOutput, calls=%fused_computation.11 | convolution fusion | flops 81264640 | bytes 16957952 | tf_op jit(solution)/shard_map/ij,rjx->rix/dot_general | solution.py:102
  (240 shorter events, 35.4 us)
Async XLA Ops:
  0.0 22.7 %copy-start = (bf16[32,64,256]{2,1,0:T(8,128)(2,1)S(1)}, bf16[32,64,256]{2,1,0:T(8,128)(2,1)}, u32[]{:S(2)}) copy-start(bf16[32,64,256]{2,1,0:T(8,128)(2,1)} %param.12) | copy-start | bytes 3145732
  2.6 22.5 %collective-permute-start = (s32[3,17]{1,0:T(4,128)S(1)}, s32[3,17]{1,0:T(4,128)S(1)}, u32[]{:S(2)}, u32[]{:S(2)}) collective-permute-start(s32[3,17]{1,0:T(4,128)S(1)} %bitcast.276), channel_id=1, source_target_pairs={{0,30},{1,31},{2,0},{3,1},{4,2},{5,3},{6,4},{7,5},{8,6},{9,7},{10,... | collective-permute-start | bytes 620 | tf_op jit(solution)/shard_map/ppermute | solution.py:10
  9.0 16.1 %collective-permute-start.1 = (s32[3,17]{1,0:T(4,128)S(1)}, s32[3,17]{1,0:T(4,128)S(1)}, u32[]{:S(2)}, u32[]{:S(2)}) collective-permute-start(s32[3,17]{1,0:T(4,128)S(1)} %bitcast.278), channel_id=1, source_target_pairs={{0,31},{1,0},{2,1},{3,2},{4,3},{5,4},{6,5},{7,6},{8,7},{9,8},{10,9... | collective-permute-start | bytes 620 | tf_op jit(solution)/shard_map/ppermute | solution.py:10
  9.0 16.1 %collective-permute-start.2 = (s32[3,17]{1,0:T(4,128)S(1)}, s32[3,17]{1,0:T(4,128)S(1)}, u32[]{:S(2)}, u32[]{:S(2)}) collective-permute-start(s32[3,17]{1,0:T(4,128)S(1)} %bitcast.280), channel_id=1, source_target_pairs={{0,1},{1,2},{2,3},{3,4},{4,5},{5,6},{6,7},{7,8},{8,9},{9,10},{10,1... | collective-permute-start | bytes 620 | tf_op jit(solution)/shard_map/ppermute | solution.py:10
  9.5 15.6 %collective-permute-start.3 = (s32[3,17]{1,0:T(4,128)S(1)}, s32[3,17]{1,0:T(4,128)S(1)}, u32[]{:S(2)}, u32[]{:S(2)}) collective-permute-start(s32[3,17]{1,0:T(4,128)S(1)} %bitcast.282), channel_id=1, source_target_pairs={{0,2},{1,3},{2,4},{3,5},{4,6},{5,7},{6,8},{7,9},{8,10},{9,11},{10,... | collective-permute-start | bytes 620 | tf_op jit(solution)/shard_map/ppermute | solution.py:10
  23.1 1.8 copy-start.3
  23.1 7.9 %copy-start.5 = (s32[1,32,4]{1,2,0:T(4,128)S(1)}, s32[1,32,4]{1,2,0:T(4,128)}, u32[]{:S(2)}) copy-start(s32[1,32,4]{1,2,0:T(4,128)} %param.13) | copy-start | bytes 1540
  25.2 5.9 %collective-permute-start.4 = (s32[5,17]{1,0:T(8,128)S(1)}, s32[5,17]{1,0:T(8,128)S(1)}, u32[]{:S(2)}, u32[]{:S(2)}) collective-permute-start(s32[5,17]{1,0:T(8,128)S(1)} %get-tuple-element.38), channel_id=1, source_target_pairs={{32,0},{64,32},{96,64},{33,1},{65,33},{97,65},{34,2},{66,34},{98,6... | collective-permute-start | bytes 1028 | tf_op jit(solution)/shard_map/ppermute | solution.py:16
  26.5 5.9 %collective-permute-start.5 = (s32[5,17]{1,0:T(8,128)S(1)}, s32[5,17]{1,0:T(8,128)S(1)}, u32[]{:S(2)}, u32[]{:S(2)}) collective-permute-start(s32[5,17]{1,0:T(8,128)S(1)} %get-tuple-element.39), channel_id=1, source_target_pairs={{0,32},{32,64},{64,96},{1,33},{33,65},{65,97},{2,34},{34,66},{66,9... | collective-permute-start | bytes 1028 | tf_op jit(solution)/shard_map/ppermute | solution.py:16
  52.3 23.3 %copy-start.6 = (f32[1,32,4]{1,2,0:T(4,128)S(1)}, f32[1,32,4]{1,2,0:T(4,128)}, u32[]{:S(2)}) copy-start(f32[1,32,4]{1,2,0:T(4,128)} %param.15) | copy-start | bytes 1540
  52.3 23.3 %copy-start.8 = (s32[1,32]{1,0:T(1,128)S(1)}, s32[1,32]{1,0:T(1,128)}, u32[]{:S(2)}) copy-start(s32[1,32]{1,0:T(1,128)} %param.16) | copy-start | bytes 388
  52.4 19.0 %collective-permute-start.6 = (bf16[17,64,256]{2,1,0:T(8,128)(2,1)S(1)}, bf16[17,64,256]{2,1,0:T(8,128)(2,1)S(1)}, u32[]{:S(2)}, u32[]{:S(2)}) collective-permute-start(bf16[17,64,256]{2,1,0:T(8,128)(2,1)S(1)} %get-tuple-element.27), channel_id=1, source_target_pairs={{0,2},{1,3},{2,4},{3,5},{4,6},{5,7},{6,8},{7,9},{8,10},{9,11},{10,... | collective-permute-start | bytes 1671176 | tf_op jit(solution)/shard_map/ppermute | solution.py:10
  52.5 24.6 %collective-permute-start.8 = (bf16[17,64,256]{2,1,0:T(8,128)(2,1)S(1)}, bf16[17,64,256]{2,1,0:T(8,128)(2,1)S(1)}, u32[]{:S(2)}, u32[]{:S(2)}) collective-permute-start(bf16[17,64,256]{2,1,0:T(8,128)(2,1)S(1)} %get-tuple-element.26), channel_id=1, source_target_pairs={{0,1},{1,2},{2,3},{3,4},{4,5},{5,6},{6,7},{7,8},{8,9},{9,10},{10,1... | collective-permute-start | bytes 1671176 | tf_op jit(solution)/shard_map/ppermute | solution.py:10
  54.3 29.7 %collective-permute-start.11 = (bf16[17,64,256]{2,1,0:T(8,128)(2,1)S(1)}, bf16[17,64,256]{2,1,0:T(8,128)(2,1)S(1)}, u32[]{:S(2)}, u32[]{:S(2)}) collective-permute-start(bf16[17,64,256]{2,1,0:T(8,128)(2,1)S(1)} %get-tuple-element.24), channel_id=1, source_target_pairs={{0,31},{1,0},{2,1},{3,2},{4,3},{5,4},{6,5},{7,6},{8,7},{9,8},{10,9... | collective-permute-start | bytes 1671176 | tf_op jit(solution)/shard_map/ppermute | solution.py:10
  71.3 17.4 %collective-permute-start.7 = (bf16[17,64,256]{2,1,0:T(8,128)(2,1)S(1)}, bf16[17,64,256]{2,1,0:T(8,128)(2,1)S(1)}, u32[]{:S(2)}, u32[]{:S(2)}) collective-permute-start(bf16[17,64,256]{2,1,0:T(8,128)(2,1)S(1)} %collective-permute-done.6), channel_id=1, source_target_pairs={{0,32},{32,64},{64,96},{1,33},{33,65},{65,97},{2,34},{34,66},{66,9... | collective-permute-start | bytes 1671176 | tf_op jit(solution)/shard_map/ppermute | solution.py:16
  75.7 18.3 %collective-permute-start.13 = (bf16[17,64,256]{2,1,0:T(8,128)(2,1)S(1)}, bf16[17,64,256]{2,1,0:T(8,128)(2,1)S(1)}, u32[]{:S(2)}, u32[]{:S(2)}) collective-permute-start(bf16[17,64,256]{2,1,0:T(8,128)(2,1)S(1)} %get-tuple-element.23), channel_id=1, source_target_pairs={{0,30},{1,31},{2,0},{3,1},{4,2},{5,3},{6,4},{7,5},{8,6},{9,7},{10,... | collective-permute-start | bytes 1671176 | tf_op jit(solution)/shard_map/ppermute | solution.py:10
  77.1 23.6 %collective-permute-start.9 = (bf16[17,64,256]{2,1,0:T(8,128)(2,1)S(1)}, bf16[17,64,256]{2,1,0:T(8,128)(2,1)S(1)}, u32[]{:S(2)}, u32[]{:S(2)}) collective-permute-start(bf16[17,64,256]{2,1,0:T(8,128)(2,1)S(1)} %collective-permute-done.8), channel_id=1, source_target_pairs={{0,32},{32,64},{64,96},{1,33},{33,65},{65,97},{2,34},{34,66},{66,9... | collective-permute-start | bytes 1671176 | tf_op jit(solution)/shard_map/ppermute | solution.py:16
  80.5 32.0 %collective-permute-start.10 = (bf16[17,64,256]{2,1,0:T(8,128)(2,1)S(1)}, bf16[17,64,256]{2,1,0:T(8,128)(2,1)S(1)}, u32[]{:S(2)}, u32[]{:S(2)}) collective-permute-start(bf16[17,64,256]{2,1,0:T(8,128)(2,1)S(1)} %get-tuple-element.25), channel_id=1, source_target_pairs={{0,32},{32,64},{64,96},{1,33},{33,65},{65,97},{2,34},{34,66},{66,9... | collective-permute-start | bytes 1671176 | tf_op jit(solution)/shard_map/ppermute | solution.py:16
  84.0 47.5 %collective-permute-start.15 = (bf16[17,64,256]{2,1,0:T(8,128)(2,1)S(1)}, bf16[17,64,256]{2,1,0:T(8,128)(2,1)S(1)}, u32[]{:S(2)}, u32[]{:S(2)}) collective-permute-start(bf16[17,64,256]{2,1,0:T(8,128)(2,1)S(1)} %get-tuple-element.22), channel_id=1, source_target_pairs={{0,2},{1,3},{2,4},{3,5},{4,6},{5,7},{6,8},{7,9},{8,10},{9,11},{10,... | collective-permute-start | bytes 1671176 | tf_op jit(solution)/shard_map/ppermute | solution.py:10
  88.7 35.8 %collective-permute-start.12 = (bf16[17,64,256]{2,1,0:T(8,128)(2,1)S(1)}, bf16[17,64,256]{2,1,0:T(8,128)(2,1)S(1)}, u32[]{:S(2)}, u32[]{:S(2)}) collective-permute-start(bf16[17,64,256]{2,1,0:T(8,128)(2,1)S(1)} %collective-permute-done.11), channel_id=1, source_target_pairs={{0,32},{32,64},{64,96},{1,33},{33,65},{65,97},{2,34},{34,66},{66,9... | collective-permute-start | bytes 1671176 | tf_op jit(solution)/shard_map/ppermute | solution.py:16
  94.0 38.5 %collective-permute-start.16 = (bf16[17,64,256]{2,1,0:T(8,128)(2,1)S(1)}, bf16[17,64,256]{2,1,0:T(8,128)(2,1)S(1)}, u32[]{:S(2)}, u32[]{:S(2)}) collective-permute-start(bf16[17,64,256]{2,1,0:T(8,128)(2,1)S(1)} %get-tuple-element.21), channel_id=1, source_target_pairs={{0,1},{1,2},{2,3},{3,4},{4,5},{5,6},{6,7},{7,8},{8,9},{9,10},{10,1... | collective-permute-start | bytes 1671176 | tf_op jit(solution)/shard_map/ppermute | solution.py:10
  100.6 30.1 %collective-permute-start.14 = (bf16[17,64,256]{2,1,0:T(8,128)(2,1)S(1)}, bf16[17,64,256]{2,1,0:T(8,128)(2,1)S(1)}, u32[]{:S(2)}, u32[]{:S(2)}) collective-permute-start(bf16[17,64,256]{2,1,0:T(8,128)(2,1)S(1)} %collective-permute-done.13), channel_id=1, source_target_pairs={{0,32},{32,64},{64,96},{1,33},{33,65},{65,97},{2,34},{34,66},{66,9... | collective-permute-start | bytes 1671176 | tf_op jit(solution)/shard_map/ppermute | solution.py:16
  112.5 24.9 %collective-permute-start.17 = (bf16[17,64,256]{2,1,0:T(8,128)(2,1)S(1)}, bf16[17,64,256]{2,1,0:T(8,128)(2,1)S(1)}, u32[]{:S(2)}, u32[]{:S(2)}) collective-permute-start(bf16[17,64,256]{2,1,0:T(8,128)(2,1)S(1)} %get-tuple-element.20), channel_id=1, source_target_pairs={{0,31},{1,0},{2,1},{3,2},{4,3},{5,4},{6,5},{7,6},{8,7},{9,8},{10,9... | collective-permute-start | bytes 1671176 | tf_op jit(solution)/shard_map/ppermute | solution.py:10
  124.5 30.1 %collective-permute-start.18 = (bf16[17,64,256]{2,1,0:T(8,128)(2,1)S(1)}, bf16[17,64,256]{2,1,0:T(8,128)(2,1)S(1)}, u32[]{:S(2)}, u32[]{:S(2)}) collective-permute-start(bf16[17,64,256]{2,1,0:T(8,128)(2,1)S(1)} %get-tuple-element.19), channel_id=1, source_target_pairs={{0,30},{1,31},{2,0},{3,1},{4,2},{5,3},{6,4},{7,5},{8,6},{9,7},{10,... | collective-permute-start | bytes 1671176 | tf_op jit(solution)/shard_map/ppermute | solution.py:10
  130.7 18.5 %collective-permute-start.19 = (bf16[17,64,256]{2,1,0:T(8,128)(2,1)S(1)}, bf16[17,64,256]{2,1,0:T(8,128)(2,1)S(1)}, u32[]{:S(2)}, u32[]{:S(2)}) collective-permute-start(bf16[17,64,256]{2,1,0:T(8,128)(2,1)S(1)} %get-tuple-element.18), channel_id=1, source_target_pairs={{0,2},{1,3},{2,4},{3,5},{4,6},{5,7},{6,8},{7,9},{8,10},{9,11},{10,... | collective-permute-start | bytes 1671176 | tf_op jit(solution)/shard_map/ppermute | solution.py:10
  131.5 20.9 %collective-permute-start.21 = (bf16[17,64,256]{2,1,0:T(8,128)(2,1)S(1)}, bf16[17,64,256]{2,1,0:T(8,128)(2,1)S(1)}, u32[]{:S(2)}, u32[]{:S(2)}) collective-permute-start(bf16[17,64,256]{2,1,0:T(8,128)(2,1)S(1)} %get-tuple-element.17), channel_id=1, source_target_pairs={{0,1},{1,2},{2,3},{3,4},{4,5},{5,6},{6,7},{7,8},{8,9},{9,10},{10,1... | collective-permute-start | bytes 1671176 | tf_op jit(solution)/shard_map/ppermute | solution.py:10
  132.4 23.5 %collective-permute-start.24 = (bf16[17,64,256]{2,1,0:T(8,128)(2,1)S(1)}, bf16[17,64,256]{2,1,0:T(8,128)(2,1)S(1)}, u32[]{:S(2)}, u32[]{:S(2)}) collective-permute-start(bf16[17,64,256]{2,1,0:T(8,128)(2,1)S(1)} %get-tuple-element.15), channel_id=1, source_target_pairs={{0,31},{1,0},{2,1},{3,2},{4,3},{5,4},{6,5},{7,6},{8,7},{9,8},{10,9... | collective-permute-start | bytes 1671176 | tf_op jit(solution)/shard_map/ppermute | solution.py:10
  137.5 19.7 %collective-permute-start.26 = (bf16[17,64,256]{2,1,0:T(8,128)(2,1)S(1)}, bf16[17,64,256]{2,1,0:T(8,128)(2,1)S(1)}, u32[]{:S(2)}, u32[]{:S(2)}) collective-permute-start(bf16[17,64,256]{2,1,0:T(8,128)(2,1)S(1)} %get-tuple-element.14), channel_id=1, source_target_pairs={{0,30},{1,31},{2,0},{3,1},{4,2},{5,3},{6,4},{7,5},{8,6},{9,7},{10,... | collective-permute-start | bytes 1671176 | tf_op jit(solution)/shard_map/ppermute | solution.py:10
  149.2 17.9 %collective-permute-start.20 = (bf16[17,64,256]{2,1,0:T(8,128)(2,1)S(1)}, bf16[17,64,256]{2,1,0:T(8,128)(2,1)S(1)}, u32[]{:S(2)}, u32[]{:S(2)}) collective-permute-start(bf16[17,64,256]{2,1,0:T(8,128)(2,1)S(1)} %collective-permute-done.19), channel_id=1, source_target_pairs={{32,0},{64,32},{96,64},{33,1},{65,33},{97,65},{34,2},{66,34},{98,6... | collective-permute-start | bytes 1671176 | tf_op jit(solution)/shard_map/ppermute | solution.py:16
  152.4 26.6 %collective-permute-start.22 = (bf16[17,64,256]{2,1,0:T(8,128)(2,1)S(1)}, bf16[17,64,256]{2,1,0:T(8,128)(2,1)S(1)}, u32[]{:S(2)}, u32[]{:S(2)}) collective-permute-start(bf16[17,64,256]{2,1,0:T(8,128)(2,1)S(1)} %collective-permute-done.21), channel_id=1, source_target_pairs={{32,0},{64,32},{96,64},{33,1},{65,33},{97,65},{34,2},{66,34},{98,6... | collective-permute-start | bytes 1671176 | tf_op jit(solution)/shard_map/ppermute | solution.py:16
  154.6 36.4 %collective-permute-start.23 = (bf16[17,64,256]{2,1,0:T(8,128)(2,1)S(1)}, bf16[17,64,256]{2,1,0:T(8,128)(2,1)S(1)}, u32[]{:S(2)}, u32[]{:S(2)}) collective-permute-start(bf16[17,64,256]{2,1,0:T(8,128)(2,1)S(1)} %get-tuple-element.16), channel_id=1, source_target_pairs={{32,0},{64,32},{96,64},{33,1},{65,33},{97,65},{34,2},{66,34},{98,6... | collective-permute-start | bytes 1671176 | tf_op jit(solution)/shard_map/ppermute | solution.py:16
  155.9 41.9 %collective-permute-start.25 = (bf16[17,64,256]{2,1,0:T(8,128)(2,1)S(1)}, bf16[17,64,256]{2,1,0:T(8,128)(2,1)S(1)}, u32[]{:S(2)}, u32[]{:S(2)}) collective-permute-start(bf16[17,64,256]{2,1,0:T(8,128)(2,1)S(1)} %collective-permute-done.24), channel_id=1, source_target_pairs={{32,0},{64,32},{96,64},{33,1},{65,33},{97,65},{34,2},{66,34},{98,6... | collective-permute-start | bytes 1671176 | tf_op jit(solution)/shard_map/ppermute | solution.py:16
  157.2 46.6 %collective-permute-start.27 = (bf16[17,64,256]{2,1,0:T(8,128)(2,1)S(1)}, bf16[17,64,256]{2,1,0:T(8,128)(2,1)S(1)}, u32[]{:S(2)}, u32[]{:S(2)}) collective-permute-start(bf16[17,64,256]{2,1,0:T(8,128)(2,1)S(1)} %collective-permute-done.26), channel_id=1, source_target_pairs={{32,0},{64,32},{96,64},{33,1},{65,33},{97,65},{34,2},{66,34},{98,6... | collective-permute-start | bytes 1671176 | tf_op jit(solution)/shard_map/ppermute | solution.py:16
  227.4 0.9 copy-start.9
  227.7 6.8 %collective-permute-start.28 = (bf16[32,64,2]{2,1,0:T(8,128)(2,1)S(1)}, bf16[32,64,2]{2,1,0:T(8,128)(2,1)S(1)}, u32[]{:S(2)}, u32[]{:S(2)}) collective-permute-start(bf16[32,64,2]{2,1,0:T(8,128)(2,1)S(1)} %get-tuple-element.32), channel_id=1, source_target_pairs={{1,0},{2,1},{3,2},{4,3},{5,4},{6,5},{7,6},{8,7},{9,8},{10,9},{11,1... | collective-permute-start | bytes 24584 | tf_op jit(solution)/shard_map/ppermute | solution.py:27
  227.8 12.0 %collective-permute-start.29 = (bf16[32,64,2]{2,1,0:T(8,128)(2,1)S(1)}, bf16[32,64,2]{2,1,0:T(8,128)(2,1)S(1)}, u32[]{:S(2)}, u32[]{:S(2)}) collective-permute-start(bf16[32,64,2]{2,1,0:T(8,128)(2,1)S(1)} %get-tuple-element.33), channel_id=1, source_target_pairs={{0,1},{1,2},{2,3},{3,4},{4,5},{5,6},{6,7},{7,8},{8,9},{9,10},{10,1... | collective-permute-start | bytes 24584 | tf_op jit(solution)/shard_map/ppermute | solution.py:26
  242.9 5.9 %collective-permute-start.30 = (bf16[1,64,256]{2,1,0:T(8,128)(2,1)S(1)}, bf16[1,64,256]{2,1,0:T(8,128)(2,1)S(1)}, u32[]{:S(2)}, u32[]{:S(2)}) collective-permute-start(bf16[1,64,256]{2,1,0:T(8,128)(2,1)S(1)} %get-tuple-element.30), channel_id=1, source_target_pairs={{0,32},{32,64},{64,96},{1,33},{33,65},{65,97},{2,34},{34,66},{66,9... | collective-permute-start | bytes 98312 | tf_op jit(solution)/shard_map/ppermute | solution.py:26
  246.6 5.8 %collective-permute-start.31 = (bf16[1,64,256]{2,1,0:T(8,128)(2,1)S(1)}, bf16[1,64,256]{2,1,0:T(8,128)(2,1)S(1)}, u32[]{:S(2)}, u32[]{:S(2)}) collective-permute-start(bf16[1,64,256]{2,1,0:T(8,128)(2,1)S(1)} %get-tuple-element.31), channel_id=1, source_target_pairs={{32,0},{64,32},{96,64},{33,1},{65,33},{97,65},{34,2},{66,34},{98,6... | collective-permute-start | bytes 98312 | tf_op jit(solution)/shard_map/ppermute | solution.py:27
  247.9 12.4 %copy-start.2 = (f32[64,32,256]{2,0,1:T(8,128)S(1)}, f32[64,32,256]{2,0,1:T(8,128)}, u32[]{:S(2)}) copy-start(f32[64,32,256]{2,0,1:T(8,128)} %fusion.27) | copy-start | bytes 6291460
  248.2 12.1 %copy-start.1 = (f32[64,32,256]{2,0,1:T(8,128)S(1)}, f32[64,32,256]{2,0,1:T(8,128)}, u32[]{:S(2)}) copy-start(f32[64,32,256]{2,0,1:T(8,128)} %fusion.26) | copy-start | bytes 6291460
  248.2 12.1 %copy-start.4 = (f32[32,256]{1,0:T(8,128)S(1)}, f32[32,256]{1,0:T(8,128)}, u32[]{:S(2)}) copy-start(f32[32,256]{1,0:T(8,128)} %param.21) | copy-start | bytes 98308
  248.2 12.1 %copy-start.7 = (f32[64]{0:T(128)S(1)}, f32[64]{0:T(128)}, u32[]{:S(2)}) copy-start(f32[64]{0:T(128)} %param.20) | copy-start | bytes 772
  248.2 6.8 %collective-permute-start.32 = (bf16[32,64,1]{2,1,0:T(8,128)(2,1)S(1)}, bf16[32,64,1]{2,1,0:T(8,128)(2,1)S(1)}, u32[]{:S(2)}, u32[]{:S(2)}) collective-permute-start(bf16[32,64,1]{2,1,0:T(8,128)(2,1)S(1)} %get-tuple-element.28), channel_id=1, source_target_pairs={{1,0},{2,1},{3,2},{4,3},{5,4},{6,5},{7,6},{8,7},{9,8},{10,9},{11,1... | collective-permute-start | bytes 12296 | tf_op jit(solution)/shard_map/ppermute | solution.py:27
  248.3 12.0 %collective-permute-start.33 = (bf16[32,64,1]{2,1,0:T(8,128)(2,1)S(1)}, bf16[32,64,1]{2,1,0:T(8,128)(2,1)S(1)}, u32[]{:S(2)}, u32[]{:S(2)}) collective-permute-start(bf16[32,64,1]{2,1,0:T(8,128)(2,1)S(1)} %get-tuple-element.29), channel_id=1, source_target_pairs={{0,1},{1,2},{2,3},{3,4},{4,5},{5,6},{6,7},{7,8},{8,9},{9,10},{10,1... | collective-permute-start | bytes 12296 | tf_op jit(solution)/shard_map/ppermute | solution.py:26
where the time goes:
time: 266 us; the launch traced here: 264 us
  waiting for transfers between devices  118 us (44%)
  starting transfers between devices  61.7 us (23%)
  local copies, waits for them, and re-layouts  61.5 us (23%)
  other arithmetic  14.2 us (5%)
  matrix products  7.62 us (3%)
    ppermute x12, waiting for transfers between devices, from_behind_2(): lax.ppermute(value, axis, [(source, source + steps) for source in range(i...  74.5 us
    ppermute x12, starting transfers between devices, from_behind_2(): lax.ppermute(value, axis, [(source, source + steps) for source in range(i...  32.3 us
    ppermute x16, starting transfers between devices, from_behind(): return lax.ppermute(value, axis, pairs)  23.4 us
    ppermute x16, waiting for transfers between devices, from_behind(): return lax.ppermute(value, axis, pairs)  20.8 us
    gather x4, local copies, waits for them, and re-layouts, body(): jnp.take(arrived, positions[:, k], axis=0).astype(jnp.float32)  19.8 us
    unnamed x40, local copies, waits for them, and re-layouts  14.9 us
    ppermute x3, waiting for transfers between devices, with_halo(): after = lax.ppermute(initial, axis, down)  12.2 us
    slice x68, local copies, waits for them, and re-layouts, toeplitz_stack(): flipped[:, bins - 1 - i:2 * bins - 1 - i]  11.6 us
  transfers between devices with their start and end apart: 34, of which 18 were waited for; matrix products, arithmetic and copies ran while one was open for 11% of the time, Pallas kernels for 0%

commit v1 on v0

v1 whole, which is shorter than its diff:
```python
import functools

import jax
import jax.numpy as jnp
from jax import lax
from jax.experimental import pallas as pl
from jax.experimental.pallas import tpu as pltpu
from jax.sharding import PartitionSpec as P

MESH = pl.DeviceIdType.MESH
ROWS = 32
BINS = 64
WIDTH = 256
ENTRIES = 4
GROUP = 16
GROUPS = BINS // GROUP
HALVES = 1
LANES = WIDTH // HALVES
CHUNKS = GROUPS * HALVES
AHEAD = 2
STRIP = 128


def kernel(
    n_lat, n_lon,
    conc, owner_v, row_v, weight_v, count_v, owner_s, row_s, weight_s, count_s, offset_s,
    rates, toeplitz, settle, kappa,
    out,
    conc_v, base, taps, toep_v, near_int, near_weight, near_count,
    own_int, near_int_s, near_weight_s, near_count_s, index_s, mix_s, scale_s,
    *rest,
):
    held = rest[0:CHUNKS]
    sent = rest[CHUNKS:2 * CHUNKS]
    got = rest[2 * CHUNKS:3 * CHUNKS]
    remapped = rest[3 * CHUNKS:3 * CHUNKS + GROUPS]
    strips = rest[3 * CHUNKS + GROUPS:3 * CHUNKS + 2 * GROUPS]
    ends = rest[3 * CHUNKS + 2 * GROUPS:3 * CHUNKS + 3 * GROUPS]
    edges = rest[3 * CHUNKS + 3 * GROUPS:3 * CHUNKS + 4 * GROUPS]
    (dep_send, dep_recv, raw_send, raw_recv, part_send, part_recv,
     strip_send, strip_recv, edge_send, edge_recv, local_sem, out_sem) = rest[3 * CHUNKS + 4 * GROUPS:]

    lat = lax.axis_index("lat")
    lon = lax.axis_index("lon")
    core = lax.rem(lon, 2)
    chip = lon - core

    def at_lon(value):
        return lax.rem(value + 2 * n_lon, n_lon)

    sibling = chip + 1 - core
    after = at_lon(chip + 2)
    before = at_lon(chip - 1)
    west, east = at_lon(lon - 1), at_lon(lon + 1)

    barrier = pltpu.get_barrier_semaphore()
    for step in (-2, -1, 1, 2):
        pl.semaphore_signal(barrier, inc=1, device_id={"lon": at_lon(lon + step)}, device_id_type=MESH)

    def with_neighbour(side, action):
        inside = lat > 0 if side == 0 else lat < n_lat - 1
        pl.when(inside)(functools.partial(action, side, lat - 1 if side == 0 else lat + 1))

    def greet(side, there):
        pl.semaphore_signal(barrier, inc=1, device_id={"lat": there}, device_id_type=MESH)

    for side in (0, 1):
        with_neighbour(side, greet)
    pl.semaphore_wait(barrier, 4 + jnp.where(lat > 0, 1, 0) + jnp.where(lat < n_lat - 1, 1, 0))

    def remote(src, dst, send, recv, **where):
        return pltpu.make_async_remote_copy(
            src_ref=src, dst_ref=dst, send_sem=send, recv_sem=recv, device_id=where, device_id_type=MESH
        )

    def window(c):
        g, h = c // HALVES, c % HALVES
        return conc.at[:, pl.ds(g * GROUP, GROUP), pl.ds(h * LANES, LANES)]

    def slot(c, number):
        return held[c].at[pl.ds(number * ROWS, ROWS)]

    def raw_sends(c):
        return [
            remote(window(c), slot(c, core), raw_send.at[c, 0], raw_recv.at[c, core], lon=after),
            remote(window(c), slot(c, core + 3), raw_send.at[c, 1], raw_recv.at[c, core], lon=before),
            remote(window(c), slot(c, 1 + 2 * core), raw_send.at[c, 2], raw_recv.at[c, 2], lon=sibling),
        ]

    far = 3 * core

    def raw_arrival(c, which):
        number = (far, far + 1, 3 - 2 * core, 4 - 4 * core)[which]
        return remote(window(c), slot(c, number), raw_send.at[c, 3], raw_recv.at[c, which], lon=sibling)

    def forward(c):
        return remote(
            slot(c, 1 + 2 * core), slot(c, 4 * core), raw_send.at[c, 3], raw_recv.at[c, 3], lon=sibling
        )

    def own_copy(c):
        return pltpu.make_async_copy(window(c), slot(c, 2), local_sem.at[c])

    def dep_sends(side, there):
        other = 1 - side
        return [
            remote(owner_v, near_int.at[other, 0], dep_send.at[side, 0], dep_recv.at[other, 0], lat=there),
            remote(row_v, near_int.at[other, 1], dep_send.at[side, 1], dep_recv.at[other, 1], lat=there),
            remote(weight_v, near_weight.at[other], dep_send.at[side, 2], dep_recv.at[other, 2], lat=there),
            remote(count_v, near_count.at[other], dep_send.at[side, 3], dep_recv.at[other, 3], lat=there),
        ]

    def dep_arrivals(side, there):
        return [
            remote(owner_v, near_int.at[side, 0], dep_send.at[side, 0], dep_recv.at[side, 0], lat=there),
            remote(row_v, near_int.at[side, 1], dep_send.at[side, 1], dep_recv.at[side, 1], lat=there),
            remote(weight_v, near_weight.at[side], dep_send.at[side, 2], dep_recv.at[side, 2], lat=there),
            remote(count_v, near_count.at[side], dep_send.at[side, 3], dep_recv.at[side, 3], lat=there),
        ]

    def start_all(make):
        def action(side, there):
            for copy in make(side, there):
                copy.start()
        return action

    for side in (0, 1):
        with_neighbour(side, start_all(dep_sends))
    for c in range(min(AHEAD, CHUNKS)):
        for copy in raw_sends(c):
            copy.start()
    whole = pltpu.make_async_copy(conc, conc_v, local_sem.at[CHUNKS])
    whole.start()
    for c in range(CHUNKS):
        own_copy(c).start()

    def clear(side):
        def action():
            for c in range(CHUNKS):
                got[c][side] = jnp.zeros((ROWS, GROUP, LANES), jnp.bfloat16)
            for g in range(GROUPS):
                edges[g][side] = jnp.zeros((GROUP, WIDTH), jnp.bfloat16)
        pl.when(lat == (0 if side == 0 else n_lat - 1))(action)

    for side in (0, 1):
        clear(side)

    toep_v[...] = jnp.zeros_like(toep_v)
    toep_v[:, pl.ds(0, 2 * BINS - 1)] = toeplitz[...].astype(jnp.float32)
    for q in range(4):
        line = jnp.broadcast_to(toep_v[pl.ds(q, 1), :], (2 * BINS, 2 * BINS))
        turned = pltpu.roll(line, BINS + 1, 1, stride=1, stride_axis=0)
        taps[pl.ds(q * BINS, BINS), :] = turned.T[:BINS, :BINS].astype(jnp.bfloat16)
    diagonal = lax.broadcasted_iota(jnp.int32, (BINS, BINS), 0) == lax.broadcasted_iota(jnp.int32, (BINS, BINS), 1)
    sinking = jnp.sum(jnp.where(diagonal, jnp.broadcast_to(settle[...], (BINS, BINS)), 0.0), axis=1, keepdims=True)
    sinking = jnp.broadcast_to(sinking, (BINS, WIDTH))

    def fill(table, group, owner, row, weight, count):
        def one(r, _):
            number = jnp.int32(0)
            masses, total = [], jnp.float32(0.0)
            for k in range(ENTRIES):
                o = owner[k, r]
                mine = (o >= 5 * group) & (o < 5 * group + 5) & (k < count[0, r])
                w = jnp.where(mine, weight[k, r], jnp.float32(0.0))
                i = jnp.where(mine, (o - 5 * group) * ROWS + row[k, r], jnp.int32(2 * ROWS))
                number = number + jnp.where(mine, jnp.int32(1), jnp.int32(0))
                masses.append((w, mine))
                total = total + w
                index_s[table, r * ENTRIES + k] = i
            for k in range(ENTRIES):
                w, mine = masses[k]
                if table < 2:
                    w = jnp.where((number == 1) & mine, jnp.float32(1.0), w)
                mix_s[table, r * ENTRIES + k] = w
            return 0
        lax.fori_loop(0, ROWS, one, 0)

    def fill_scale(r, _):
        for side in (0, 1):
            group = 2 * side
            number, total = jnp.int32(0), jnp.float32(0.0)
            for k in range(ENTRIES):
                o = owner_s[k, r]
                mine = (o >= 5 * group) & (o < 5 * group + 5) & (k < count_s[0, r])
                number = number + jnp.where(mine, jnp.int32(1), jnp.int32(0))
                total = total + jnp.where(mine, weight_s[k, r], jnp.float32(0.0))
            scale_s[side, r] = jnp.where(number == 1, total, jnp.float32(1.0))
        return 0

    fill(2, 1, owner_s, row_s, weight_s, count_s)
    lax.fori_loop(0, ROWS, fill_scale, 0)

    def read_near(side, there):
        for copy in dep_arrivals(side, there):
            copy.wait_recv()
        moves = [
            pltpu.make_async_copy(near_int.at[side], near_int_s.at[side], own_int.at[side, 0]),
            pltpu.make_async_copy(near_weight.at[side], near_weight_s.at[side], own_int.at[side, 1]),
            pltpu.make_async_copy(near_count.at[side], near_count_s.at[side], own_int.at[side, 2]),
        ]
        for move in moves:
            move.start()
        for move in moves:
            move.wait()
        fill(side, 2 - 2 * side, near_int_s.at[side, 0], near_int_s.at[side, 1], near_weight_s.at[side],
             near_count_s.at[side])

    for side in (0, 1):
        with_neighbour(side, read_near)

    whole.wait()

    def grow(r, _):
        cells = conc_v[r]
        product = jnp.dot(taps[...], cells, preferred_element_type=jnp.float32)
        total = -sinking * cells.astype(jnp.float32)
        for q in range(4):
            total = total + rates[q, pl.ds(r, 1), :] * product[q * BINS:(q + 1) * BINS]
        base[r] = total
        return 0

    lax.fori_loop(0, ROWS, grow, 0)

    def mixed(c, table, r):
        total = jnp.zeros((GROUP, LANES), jnp.float32)
        for k in range(ENTRIES):
            place = index_s[table, r * ENTRIES + k]
            total = total + mix_s[table, r * ENTRIES + k] * held[c][place].astype(jnp.float32)
        return total

    def part_send_copy(c, side, there):
        return remote(
            sent[c].at[side], got[c].at[1 - side], part_send.at[c, side], part_recv.at[c, 1 - side], lat=there
        )

    def part_arrival(c, side, there):
        return remote(
            sent[c].at[side], got[c].at[side], part_send.at[c, side], part_recv.at[c, side], lat=there
        )

    def partials(c):
        def action(side, there):
            def one(r, _):
                sent[c][side, r] = mixed(c, side, r).astype(jnp.bfloat16)
                return 0
            lax.fori_loop(0, ROWS, one, 0, unroll=2)
            part_send_copy(c, side, there).start()
        for side in (0, 1):
            with_neighbour(side, action)

    def remap(c):
        g, h = c // HALVES, c % HALVES
        for side in (0, 1):
            with_neighbour(side, lambda side, there: part_arrival(c, side, there).wait_recv())

        def one(r, _):
            total = mixed(c, 2, r)
            for side in (0, 1):
                total = total + scale_s[side, r] * got[c][side, r].astype(jnp.float32)
            remapped[g][r, :, pl.ds(h * LANES, LANES)] = total.astype(jnp.bfloat16)
            return 0

        lax.fori_loop(0, ROWS, one, 0, unroll=2)

    def strip_sends(g):
        return [
            remote(remapped[g].at[:, :, pl.ds(0, STRIP)], strips[g].at[1],
                   strip_send.at[g, 0], strip_recv.at[g, 1], lon=west),
            remote(remapped[g].at[:, :, pl.ds(WIDTH - STRIP, STRIP)], strips[g].at[0],
                   strip_send.at[g, 1], strip_recv.at[g, 0], lon=east),
        ]

    def strip_arrivals(g):
        return [
            remote(remapped[g].at[:, :, pl.ds(0, STRIP)], strips[g].at[side],
                   strip_send.at[g, side], strip_recv.at[g, side], lon=west)
            for side in (0, 1)
        ]

    span = WIDTH + 2 * STRIP

    def shifted(g, r):
        line = jnp.concatenate([strips[g][0, r], remapped[g][r], strips[g][1, r]], axis=1).astype(jnp.float32)
        step = offset_s[r]
        line = pltpu.roll(line, jnp.where(step < 0, step + span, step), 1)
        beside = pltpu.roll(line, 1, 1) + pltpu.roll(line, span - 1, 1)
        return line[:, STRIP:STRIP + WIDTH], beside[:, STRIP:STRIP + WIDTH]

    def edge_copy(g, side, there):
        return remote(
            ends[g].at[side], edges[g].at[1 - side], edge_send.at[g, side], edge_recv.at[g, 1 - side], lat=there
        )

    def edge_arrival(g, side, there):
        return remote(
            ends[g].at[side], edges[g].at[side], edge_send.at[g, side], edge_recv.at[g, side], lat=there
        )

    def outer_rows(g):
        for copy in strip_arrivals(g):
            copy.wait_recv()

        def action(side, there):
            center, _ = shifted(g, 0 if side == 0 else ROWS - 1)
            ends[g][side] = center.astype(jnp.bfloat16)
            edge_copy(g, side, there).start()

        for side in (0, 1):
            with_neighbour(side, action)

    def out_copy(g):
        return pltpu.make_async_copy(
            base.at[:, pl.ds(g * GROUP, GROUP), :], out.at[:, pl.ds(g * GROUP, GROUP), :], out_sem.at[g]
        )

    def finish(g):
        for side in (0, 1):
            with_neighbour(side, lambda side, there: edge_arrival(g, side, there).wait_recv())

        def emit(r, above, center, beside, below):
            total = base[r, pl.ds(g * GROUP, GROUP), :] + center
            base[r, pl.ds(g * GROUP, GROUP), :] = total + kappa[pl.ds(r, 1), :] * (
                (above + below) + beside - 4.0 * center
            )

        def one(r, carry):
            above, center, beside = carry
            below, below_beside = shifted(g, r + 1)
            emit(r, above, center, beside, below)
            return center, below, below_beside

        center, beside = shifted(g, 0)
        above = edges[g][0].astype(jnp.float32)
        above, center, beside = lax.fori_loop(0, ROWS - 1, one, (above, center, beside))
        emit(ROWS - 1, above, center, beside, edges[g][1].astype(jnp.float32))
        out_copy(g).start()

    for c in range(CHUNKS):
        for which in (0, 1):
            raw_arrival(c, which).wait_recv()
        forward(c).start()
        if c + AHEAD < CHUNKS:
            for copy in raw_sends(c + AHEAD):
                copy.start()
        own_copy(c).wait()
        for which in (2, 3):
            raw_arrival(c, which).wait_recv()
        partials(c)
        if c >= 1:
            remap(c - 1)
            if (c - 1) % HALVES == HALVES - 1:
                for copy in strip_sends((c - 1) // HALVES):
                    copy.start()
        if c % HALVES == 0 and c // HALVES >= 2:
            outer_rows(c // HALVES - 2)
        if c % HALVES == 0 and c // HALVES >= 3:
            finish(c // HALVES - 3)
    if GROUPS >= 3:
        finish(GROUPS - 3)
    outer_rows(GROUPS - 2)
    remap(CHUNKS - 1)
    for copy in strip_sends(GROUPS - 1):
        copy.start()
    finish(GROUPS - 2)
    outer_rows(GROUPS - 1)
    finish(GROUPS - 1)

    for c in range(CHUNKS):
        for copy in raw_sends(c):
            copy.wait_send()
        forward(c).wait_send()
        for side in (0, 1):
            with_neighbour(side, lambda side, there: part_send_copy(c, side, there).wait_send())
    for g in range(GROUPS):
        for copy in strip_sends(g):
            copy.wait_send()
        for side in (0, 1):
            with_neighbour(side, lambda side, there: edge_copy(g, side, there).wait_send())
        out_copy(g).wait()

    def dep_sent(side, there):
        for copy in dep_sends(side, there):
            copy.wait_send()

    for side in (0, 1):
        with_neighbour(side, dep_sent)


def solution(mesh):
    n_lat, n_lon = mesh.shape["lat"], mesh.shape["lon"]

    def body(conc, dep_owner, dep_row, dep_weight, dep_count, zonal_offset, agg_rates, toeplitz, settle, kappa):
        owner, row, weight = dep_owner[0].T, dep_row[0].T, dep_weight[0].T
        any_space = pl.BlockSpec(memory_space=pl.ANY)
        vmem = pl.BlockSpec(memory_space=pltpu.VMEM)
        smem = pl.BlockSpec(memory_space=pltpu.SMEM)
        bf16, f32, i32 = jnp.bfloat16, jnp.float32, jnp.int32
        dma = pltpu.SemaphoreType.DMA
        return pl.pallas_call(
            functools.partial(kernel, n_lat, n_lon),
            out_shape=jax.ShapeDtypeStruct((ROWS, BINS, WIDTH), f32),
            in_specs=[any_space, vmem, vmem, vmem, vmem, smem, smem, smem, smem, smem, vmem, vmem, vmem, vmem],
            out_specs=any_space,
            scratch_shapes=[
                pltpu.VMEM((ROWS, BINS, WIDTH), bf16),
                pltpu.VMEM((ROWS, BINS, WIDTH), f32),
                pltpu.VMEM((4 * BINS, BINS), bf16),
                pltpu.VMEM((4, 2 * BINS), f32),
                pltpu.VMEM((2, 2, ENTRIES, ROWS), i32),
                pltpu.VMEM((2, ENTRIES, ROWS), f32),
                pltpu.VMEM((2, 1, ROWS), i32),
                dma((2, 3)),
                pltpu.SMEM((2, 2, ENTRIES, ROWS), i32),
                pltpu.SMEM((2, ENTRIES, ROWS), f32),
                pltpu.SMEM((2, 1, ROWS), i32),
                pltpu.SMEM((3, ROWS * ENTRIES), i32),
                pltpu.SMEM((3, ROWS * ENTRIES), f32),
                pltpu.SMEM((2, ROWS), f32),
            ]
            + [pltpu.VMEM((5 * ROWS, GROUP, LANES), bf16) for _ in range(CHUNKS)]
            + [pltpu.VMEM((2, ROWS, GROUP, LANES), bf16) for _ in range(2 * CHUNKS)]
            + [pltpu.VMEM((ROWS, GROUP, WIDTH), bf16) for _ in range(GROUPS)]
            + [pltpu.VMEM((2, ROWS, GROUP, STRIP), bf16) for _ in range(GROUPS)]
            + [pltpu.VMEM((2, GROUP, WIDTH), bf16) for _ in range(2 * GROUPS)]
            + [
                dma((2, 4)), dma((2, 4)),
                dma((CHUNKS, 4)), dma((CHUNKS, 4)),
                dma((CHUNKS, 2)), dma((CHUNKS, 2)),
                dma((GROUPS, 2)), dma((GROUPS, 2)),
                dma((GROUPS, 2)), dma((GROUPS, 2)),
                dma((CHUNKS + 1,)), dma((GROUPS,)),
            ],
            compiler_params=pltpu.CompilerParams(
                collective_id=0, has_side_effects=True, vmem_limit_bytes=40 << 20
            ),
            name="remap_step",
        )(
            conc, owner, row, weight, dep_count, owner, row, weight, dep_count, zonal_offset,
            agg_rates, toeplitz, settle.reshape(1, BINS), kappa,
        )

    return jax.shard_map(
        body,
        mesh=mesh,
        in_specs=(
            P("lat", None, "lon"),
            P("lon", "lat", None),
            P("lon", "lat", None),
            P("lon", "lat", None),
            P("lon", "lat"),
            P("lat"),
            P(None, "lat", "lon"),
            P(),
            P(),
            P("lat", "lon"),
        ),
        out_specs=P("lat", None, "lon"),
        check_vma=False,
    )
```

time: 266 us -> 76.8 us (0.29)
  waiting for transfers between devices: 118 us -> 0 us
  Pallas kernels: 0 us -> 67.5 us
  starting transfers between devices: 61.7 us -> 0 us
  local copies, waits for them, and re-layouts: 61.5 us -> 8.89 us
  other arithmetic: 14.2 us -> 0 us
  matrix products: 7.62 us -> 0 us
    ppermute x34 -> x0, waiting for transfers between devices: 118 us -> none  [the longest x12 74.5 us: from_behind_2(): lax.ppermute(value, axis, [(source, source + steps) for source in range(i...]
    pallas_call x0 -> x1, Pallas kernels: none -> 67.5 us  [body(): pl.pallas_call(functools.partial(kernel, n_lat, n_lon), out_shape=jax.Sha...]
    ppermute x34 -> x0, starting transfers between devices: 61.7 us -> none  [the longest x12 32.3 us: from_behind_2(): lax.ppermute(value, axis, [(source, source + steps) for source in range(i...]
    gather x5 -> x0, local copies, waits for them, and re-layouts: 28.3 us -> none  [the longest x4 19.8 us: body(): jnp.take(arrived, positions[:, k], axis=0).astype(jnp.float32)]
    slice x72 -> x0, local copies, waits for them, and re-layouts: 12.1 us -> none  [the longest x68 11.6 us: toeplitz_stack(): flipped[:, bins - 1 - i:2 * bins - 1 - i]]
    dot_general x5 -> x0, matrix products: 7.62 us -> none  [the longest x4 7.32 us: body(): jnp.einsum('ij,rjx->rix', matrices[q], conc, preferred_element_type=jnp.f...]
    select_n x3 -> x0, other arithmetic: 7.49 us -> none  [the longest x2 7.49 us: body(): jnp.take(conc, wanted.reshape(-1), axis=0)]
    unnamed x40 -> x21, local copies, waits for them, and re-layouts: 14.9 us -> 8.89 us
  transfers between devices with their start and end apart: 34 -> 0, of which waited for: 18 -> 0; matrix products, arithmetic and copies ran while one was open for 11% -> 0% of each run, Pallas kernels for 0% -> 0%
where the time goes in v1:
time: 76.8 us; the launch traced here: 76.5 us
  Pallas kernels  67.5 us (88%)
  local copies, waits for them, and re-layouts  8.89 us (12%)
    pallas_call x1, Pallas kernels, body(): pl.pallas_call(functools.partial(kernel, n_lat, n_lon), out_shape=jax.Sha...  67.5 us
    unnamed x21, local copies, waits for them, and re-layouts  8.89 us

profile of v1, /device:TPU:0, one launch (start us, length us, event | category | flops | bytes accessed | tf_op | source)
XLA Modules:
  0.0 76.5 jit_solution(502156429382734523)
XLA Ops:
  0.0 0.0 copy-start
  0.0 1.2 %copy-done = bf16[32,64,256]{2,1,0:T(8,128)(2,1)S(1)} copy-done((bf16[32,64,256]{2,1,0:T(8,128)(2,1)S(1)}, bf16[32,64,256]{2,1,0:T(8,128)(2,1)}, u32[]{:S(2)}) %copy-start) | copy-done | bytes 1048600
  1.2 0.0 copy-start.1
  1.2 0.9 %copy-done.1 = f32[4,32,256]{2,1,0:T(8,128)S(1)} copy-done((f32[4,32,256]{2,1,0:T(8,128)S(1)}, f32[4,32,256]{2,1,0:T(8,128)}, u32[]{:S(2)}) %copy-start.1) | copy-done | bytes 131096
  2.1 0.0 copy-start.2
  2.1 0.8 copy-done.2
  2.9 0.0 copy-start.3
  2.9 0.7 copy-done.3
  3.6 0.0 copy-start.4
  3.6 0.7 copy-done.4
  4.3 0.0 copy-start.5
  4.3 0.7 copy-done.5
  4.9 0.0 copy-start.6
  4.9 0.7 copy-done.6
  5.6 0.0 copy-start.7
  5.6 0.7 copy-done.7
  6.3 0.0 copy-start.8
  6.3 0.7 copy-done.8
  6.9 0.0 copy-start.9
  6.9 0.7 copy-done.9
  7.6 67.5 %remap_step.1 = f32[32,64,256]{2,1,0:T(8,128)S(1)} custom-call(bf16[32,64,256]{2,1,0:T(8,128)(2,1)S(1)} %copy-done, s32[4,32]{1,0:T(4,128)S(1)} %bitcast.10, s32[4,32]{1,0:T(4,128)S(1)} %bitcast.12, f32[4,32]{1,0:T(4,128)S(1)} %bitcast.14, s32[1,32]{1,0:T(1,128)S(1)} %copy-done.6, s32[4,32]{1,0:T(4,128)S(1)} %bitcast.11, s32[4,32]{1,0:T(4,128)S(1)} %bitcast.13, ...), custom_call_target="tpu_custom_call" | custom-call | tf_op jit(solution)/shard_map/remap_step/pallas_call | solution.py:400
  75.1 1.3 %copy.12 = f32[32,64,256]{2,1,0:T(8,128)} copy(f32[32,64,256]{2,1,0:T(8,128)S(1)} %remap_step.1) | data formatting | bytes 4194304
Async XLA Ops:
  0.0 1.2 %copy-start = (bf16[32,64,256]{2,1,0:T(8,128)(2,1)S(1)}, bf16[32,64,256]{2,1,0:T(8,128)(2,1)}, u32[]{:S(2)}) copy-start(bf16[32,64,256]{2,1,0:T(8,128)(2,1)} %conc.1) | copy-start | bytes 3145732
  1.2 0.9 %copy-start.1 = (f32[4,32,256]{2,1,0:T(8,128)S(1)}, f32[4,32,256]{2,1,0:T(8,128)}, u32[]{:S(2)}) copy-start(f32[4,32,256]{2,1,0:T(8,128)} %rates.1) | copy-start | bytes 393220
  2.1 0.8 copy-start.2
  2.9 0.7 copy-start.3
  3.6 0.7 copy-start.4
  4.3 0.7 copy-start.5
  4.9 0.7 copy-start.6
  5.6 0.7 copy-start.7
  6.3 0.7 copy-start.8
  6.9 0.7 copy-start.9

commit v2 on v1

--- a/solution.py
+++ b/solution.py
@@ -23,11 +23,11 @@
 
 def kernel(
     n_lat, n_lon,
-    conc, owner_v, row_v, weight_v, count_v, owner_s, row_s, weight_s, count_s, offset_s,
-    rates, toeplitz, settle, kappa,
-    out,
-    conc_v, base, taps, toep_v, near_int, near_weight, near_count,
-    own_int, near_int_s, near_weight_s, near_count_s, index_s, mix_s, scale_s,
+    conc, owner_h, row_h, weight_h, count_h, offset_h, rates_h, toeplitz_h, settle_h, kappa_h,
+    base,
+    owner_s, row_s, weight_s, count_s, offset_s, rates, toeplitz, settle, kappa,
+    conc_v, taps, toep_v, near_int, near_weight, near_count,
+    fetch_sem, own_int, near_int_s, near_weight_s, near_count_s, index_s, mix_s, scale_s,
     *rest,
 ):
     held = rest[0:CHUNKS]
@@ -38,7 +38,7 @@
     ends = rest[3 * CHUNKS + 2 * GROUPS:3 * CHUNKS + 3 * GROUPS]
     edges = rest[3 * CHUNKS + 3 * GROUPS:3 * CHUNKS + 4 * GROUPS]
     (dep_send, dep_recv, raw_send, raw_recv, part_send, part_recv,
-     strip_send, strip_recv, edge_send, edge_recv, local_sem, out_sem) = rest[3 * CHUNKS + 4 * GROUPS:]
+     strip_send, strip_recv, edge_send, edge_recv, local_sem) = rest[3 * CHUNKS + 4 * GROUPS:]
 
     lat = lax.axis_index("lat")
     lon = lax.axis_index("lon")
@@ -52,6 +52,16 @@
     after = at_lon(chip + 2)
     before = at_lon(chip - 1)
     west, east = at_lon(lon - 1), at_lon(lon + 1)
+
+    fetches = [
+        pltpu.make_async_copy(src, dst, fetch_sem.at[i])
+        for i, (src, dst) in enumerate([
+            (owner_h, owner_s), (row_h, row_s), (weight_h, weight_s), (count_h, count_s), (offset_h, offset_s),
+            (toeplitz_h, toeplitz), (settle_h, settle), (rates_h, rates), (kappa_h, kappa), (conc, conc_v),
+        ])
+    ]
+    for fetch in fetches:
+        fetch.start()
 
     barrier = pltpu.get_barrier_semaphore()
     for step in (-2, -1, 1, 2):
@@ -104,18 +114,18 @@
     def dep_sends(side, there):
         other = 1 - side
         return [
-            remote(owner_v, near_int.at[other, 0], dep_send.at[side, 0], dep_recv.at[other, 0], lat=there),
-            remote(row_v, near_int.at[other, 1], dep_send.at[side, 1], dep_recv.at[other, 1], lat=there),
-            remote(weight_v, near_weight.at[other], dep_send.at[side, 2], dep_recv.at[other, 2], lat=there),
-            remote(count_v, near_count.at[other], dep_send.at[side, 3], dep_recv.at[other, 3], lat=there),
+            remote(owner_h, near_int.at[other, 0], dep_send.at[side, 0], dep_recv.at[other, 0], lat=there),
+            remote(row_h, near_int.at[other, 1], dep_send.at[side, 1], dep_recv.at[other, 1], lat=there),
+            remote(weight_h, near_weight.at[other], dep_send.at[side, 2], dep_recv.at[other, 2], lat=there),
+            remote(count_h, near_count.at[other], dep_send.at[side, 3], dep_recv.at[other, 3], lat=there),
         ]
 
     def dep_arrivals(side, there):
         return [
-            remote(owner_v, near_int.at[side, 0], dep_send.at[side, 0], dep_recv.at[side, 0], lat=there),
-            remote(row_v, near_int.at[side, 1], dep_send.at[side, 1], dep_recv.at[side, 1], lat=there),
-            remote(weight_v, near_weight.at[side], dep_send.at[side, 2], dep_recv.at[side, 2], lat=there),
-            remote(count_v, near_count.at[side], dep_send.at[side, 3], dep_recv.at[side, 3], lat=there),
+            remote(owner_h, near_int.at[side, 0], dep_send.at[side, 0], dep_recv.at[side, 0], lat=there),
+            remote(row_h, near_int.at[side, 1], dep_send.at[side, 1], dep_recv.at[side, 1], lat=there),
+            remote(weight_h, near_weight.at[side], dep_send.at[side, 2], dep_recv.at[side, 2], lat=there),
+            remote(count_h, near_count.at[side], dep_send.at[side, 3], dep_recv.at[side, 3], lat=there),
         ]
 
     def start_all(make):
@@ -129,8 +139,6 @@
     for c in range(min(AHEAD, CHUNKS)):
         for copy in raw_sends(c):
             copy.start()
-    whole = pltpu.make_async_copy(conc, conc_v, local_sem.at[CHUNKS])
-    whole.start()
     for c in range(CHUNKS):
         own_copy(c).start()
 
@@ -144,6 +152,9 @@
 
     for side in (0, 1):
         clear(side)
+
+    for fetch in fetches[5:7]:
+        fetch.wait()
 
     toep_v[...] = jnp.zeros_like(toep_v)
     toep_v[:, pl.ds(0, 2 * BINS - 1)] = toeplitz[...].astype(jnp.float32)
@@ -188,6 +199,8 @@
             scale_s[side, r] = jnp.where(number == 1, total, jnp.float32(1.0))
         return 0
 
+    for fetch in fetches[:5]:
+        fetch.wait()
     fill(2, 1, owner_s, row_s, weight_s, count_s)
     lax.fori_loop(0, ROWS, fill_scale, 0)
 
@@ -209,7 +222,8 @@
     for side in (0, 1):
         with_neighbour(side, read_near)
 
-    whole.wait()
+    for fetch in fetches[7:]:
+        fetch.wait()
 
     def grow(r, _):
         cells = conc_v[r]
@@ -309,11 +323,6 @@
         for side in (0, 1):
             with_neighbour(side, action)
 
-    def out_copy(g):
-        return pltpu.make_async_copy(
-            base.at[:, pl.ds(g * GROUP, GROUP), :], out.at[:, pl.ds(g * GROUP, GROUP), :], out_sem.at[g]
-        )
-
     def finish(g):
         for side in (0, 1):
             with_neighbour(side, lambda side, there: edge_arrival(g, side, there).wait_recv())
@@ -334,7 +343,6 @@
         above = edges[g][0].astype(jnp.float32)
         above, center, beside = lax.fori_loop(0, ROWS - 1, one, (above, center, beside))
         emit(ROWS - 1, above, center, beside, edges[g][1].astype(jnp.float32))
-        out_copy(g).start()
 
     for c in range(CHUNKS):
         for which in (0, 1):
@@ -377,7 +385,6 @@
             copy.wait_send()
         for side in (0, 1):
             with_neighbour(side, lambda side, there: edge_copy(g, side, there).wait_send())
-        out_copy(g).wait()
 
     def dep_sent(side, there):
         for copy in dep_sends(side, there):
@@ -392,24 +399,31 @@
 
     def body(conc, dep_owner, dep_row, dep_weight, dep_count, zonal_offset, agg_rates, toeplitz, settle, kappa):
         owner, row, weight = dep_owner[0].T, dep_row[0].T, dep_weight[0].T
-        any_space = pl.BlockSpec(memory_space=pl.ANY)
-        vmem = pl.BlockSpec(memory_space=pltpu.VMEM)
-        smem = pl.BlockSpec(memory_space=pltpu.SMEM)
+        hbm = pl.BlockSpec(memory_space=pltpu.HBM)
         bf16, f32, i32 = jnp.bfloat16, jnp.float32, jnp.int32
         dma = pltpu.SemaphoreType.DMA
         return pl.pallas_call(
             functools.partial(kernel, n_lat, n_lon),
             out_shape=jax.ShapeDtypeStruct((ROWS, BINS, WIDTH), f32),
-            in_specs=[any_space, vmem, vmem, vmem, vmem, smem, smem, smem, smem, smem, vmem, vmem, vmem, vmem],
-            out_specs=any_space,
+            in_specs=[hbm] * 10,
+            out_specs=pl.BlockSpec(memory_space=pltpu.VMEM),
             scratch_shapes=[
+                pltpu.SMEM((ENTRIES, ROWS), i32),
+                pltpu.SMEM((ENTRIES, ROWS), i32),
+                pltpu.SMEM((ENTRIES, ROWS), f32),
+                pltpu.SMEM((1, ROWS), i32),
+                pltpu.SMEM((ROWS,), i32),
+                pltpu.VMEM((4, ROWS, WIDTH), f32),
+                pltpu.VMEM((4, 2 * BINS - 1), bf16),
+                pltpu.VMEM((1, BINS), f32),
+                pltpu.VMEM((ROWS, WIDTH), f32),
                 pltpu.VMEM((ROWS, BINS, WIDTH), bf16),
-                pltpu.VMEM((ROWS, BINS, WIDTH), f32),
                 pltpu.VMEM((4 * BINS, BINS), bf16),
                 pltpu.VMEM((4, 2 * BINS), f32),
                 pltpu.VMEM((2, 2, ENTRIES, ROWS), i32),
                 pltpu.VMEM((2, ENTRIES, ROWS), f32),
                 pltpu.VMEM((2, 1, ROWS), i32),
+                dma((10,)),
                 dma((2, 3)),
                 pltpu.SMEM((2, 2, ENTRIES, ROWS), i32),
                 pltpu.SMEM((2, ENTRIES, ROWS), f32),
@@ -429,15 +443,20 @@
                 dma((CHUNKS, 2)), dma((CHUNKS, 2)),
                 dma((GROUPS, 2)), dma((GROUPS, 2)),
                 dma((GROUPS, 2)), dma((GROUPS, 2)),
-                dma((CHUNKS + 1,)), dma((GROUPS,)),
+                dma((CHUNKS,)),
             ],
             compiler_params=pltpu.CompilerParams(
                 collective_id=0, has_side_effects=True, vmem_limit_bytes=40 << 20
             ),
             name="remap_step",
         )(
-            conc, owner, row, weight, dep_count, owner, row, weight, dep_count, zonal_offset,
-            agg_rates, toeplitz, settle.reshape(1, BINS), kappa,
+            *[
+                pltpu.with_memory_space_constraint(operand, pltpu.HBM)
+                for operand in (
+                    conc, owner, row, weight, dep_count, zonal_offset, agg_rates, toeplitz,
+                    settle.reshape(1, BINS), kappa,
+                )
+            ]
         )
 
     return jax.shard_map(

time: 76.8 us -> 68.3 us (0.89)
  local copies, waits for them, and re-layouts: 8.89 us -> 1.32 us
    unnamed x21 -> x1, local copies, waits for them, and re-layouts: 8.89 us -> 1.32 us
where the time goes in v2:
time: 68.3 us; the launch traced here: 68.2 us
  Pallas kernels  66.8 us (98%)
  local copies, waits for them, and re-layouts  1.32 us (2%)
    pallas_call x1, Pallas kernels, body(): pl.pallas_call(functools.partial(kernel, n_lat, n_lon), out_shape=jax.Sha...  66.8 us

profile of v2, /device:TPU:0, one launch (start us, length us, event | category | flops | bytes accessed | tf_op | source)
XLA Modules:
  0.0 68.2 jit_solution(3655293285219285669)
XLA Ops:
  0.0 66.8 %remap_step.1 = f32[32,64,256]{2,1,0:T(8,128)S(1)} custom-call(bf16[32,64,256]{2,1,0:T(8,128)(2,1)} %conc.1, s32[4,32]{1,0:T(4,128)} %bitcast.10, s32[4,32]{1,0:T(4,128)} %bitcast.11, f32[4,32]{1,0:T(4,128)} %bitcast.12, s32[1,32]{1,0:T(1,128)} %count_h.1, s32[32]{0:T(128)} %offset_h.1, f32[4,32,256]{2,1,0:T(8,128)} %rates_h.1, bf16[4,127]{1,0:T(4,128)(2,1)} %toeplitz_h.1, ...), custom_call_target="tpu_custom_call" | custom-call | tf_op jit(solution)/shard_map/remap_step/pallas_call | solution.py:405
  66.8 1.3 %copy.12 = f32[32,64,256]{2,1,0:T(8,128)} copy(f32[32,64,256]{2,1,0:T(8,128)S(1)} %remap_step.1) | data formatting | bytes 4194304

commit v3 on v2

--- a/solution.py
+++ b/solution.py
@@ -37,8 +37,10 @@
     strips = rest[3 * CHUNKS + GROUPS:3 * CHUNKS + 2 * GROUPS]
     ends = rest[3 * CHUNKS + 2 * GROUPS:3 * CHUNKS + 3 * GROUPS]
     edges = rest[3 * CHUNKS + 3 * GROUPS:3 * CHUNKS + 4 * GROUPS]
+    centers = rest[3 * CHUNKS + 4 * GROUPS:3 * CHUNKS + 5 * GROUPS]
+    besides = rest[3 * CHUNKS + 5 * GROUPS:3 * CHUNKS + 6 * GROUPS]
     (dep_send, dep_recv, raw_send, raw_recv, part_send, part_recv,
-     strip_send, strip_recv, edge_send, edge_recv, local_sem) = rest[3 * CHUNKS + 4 * GROUPS:]
+     strip_send, strip_recv, edge_send, edge_recv, local_sem) = rest[3 * CHUNKS + 6 * GROUPS:]
 
     lat = lax.axis_index("lat")
     lon = lax.axis_index("lon")
@@ -234,7 +236,8 @@
         base[r] = total
         return 0
 
-    lax.fori_loop(0, ROWS, grow, 0)
+    def grow_some(c):
+        lax.fori_loop(c * (ROWS // CHUNKS), (c + 1) * (ROWS // CHUNKS), grow, 0, unroll=2)
 
     def mixed(c, table, r):
         total = jnp.zeros((GROUP, LANES), jnp.float32)
@@ -323,26 +326,26 @@
         for side in (0, 1):
             with_neighbour(side, action)
 
+        def one(r, _):
+            centers[g][r + 1], besides[g][r] = shifted(g, r)
+            return 0
+
+        lax.fori_loop(0, ROWS, one, 0, unroll=4)
+
     def finish(g):
         for side in (0, 1):
             with_neighbour(side, lambda side, there: edge_arrival(g, side, there).wait_recv())
-
-        def emit(r, above, center, beside, below):
-            total = base[r, pl.ds(g * GROUP, GROUP), :] + center
-            base[r, pl.ds(g * GROUP, GROUP), :] = total + kappa[pl.ds(r, 1), :] * (
-                (above + below) + beside - 4.0 * center
-            )
-
-        def one(r, carry):
-            above, center, beside = carry
-            below, below_beside = shifted(g, r + 1)
-            emit(r, above, center, beside, below)
-            return center, below, below_beside
-
-        center, beside = shifted(g, 0)
-        above = edges[g][0].astype(jnp.float32)
-        above, center, beside = lax.fori_loop(0, ROWS - 1, one, (above, center, beside))
-        emit(ROWS - 1, above, center, beside, edges[g][1].astype(jnp.float32))
+        centers[g][0] = edges[g][0].astype(jnp.float32)
+        centers[g][ROWS + 1] = edges[g][1].astype(jnp.float32)
+        bins = pl.ds(g * GROUP, GROUP)
+
+        def one(r, _):
+            center = centers[g][r + 1]
+            around = (centers[g][r] + centers[g][r + 2]) + besides[g][r]
+            base[r, bins, :] = base[r, bins, :] + center + kappa[pl.ds(r, 1), :] * (around - 4.0 * center)
+            return 0
+
+        lax.fori_loop(0, ROWS, one, 0, unroll=4)
 
     for c in range(CHUNKS):
         for which in (0, 1):
@@ -355,6 +358,7 @@
         for which in (2, 3):
             raw_arrival(c, which).wait_recv()
         partials(c)
+        grow_some(c)
         if c >= 1:
             remap(c - 1)
             if (c - 1) % HALVES == HALVES - 1:
@@ -437,6 +441,8 @@
             + [pltpu.VMEM((ROWS, GROUP, WIDTH), bf16) for _ in range(GROUPS)]
             + [pltpu.VMEM((2, ROWS, GROUP, STRIP), bf16) for _ in range(GROUPS)]
             + [pltpu.VMEM((2, GROUP, WIDTH), bf16) for _ in range(2 * GROUPS)]
+            + [pltpu.VMEM((ROWS + 2, GROUP, WIDTH), f32) for _ in range(GROUPS)]
+            + [pltpu.VMEM((ROWS, GROUP, WIDTH), f32) for _ in range(GROUPS)]
             + [
                 dma((2, 4)), dma((2, 4)),
                 dma((CHUNKS, 4)), dma((CHUNKS, 4)),

time: 68.3 us -> 55.1 us (0.81)
  Pallas kernels: 66.8 us -> 53.7 us
    pallas_call x1, Pallas kernels: 66.8 us -> 53.7 us  [body(): pl.pallas_call(functools.partial(kernel, n_lat, n_lon), out_shape=jax.Sha...]
where the time goes in v3:
time: 55.1 us; the launch traced here: 55 us
  Pallas kernels  53.7 us (97%)
  local copies, waits for them, and re-layouts  1.32 us (2%)
    pallas_call x1, Pallas kernels, body(): pl.pallas_call(functools.partial(kernel, n_lat, n_lon), out_shape=jax.Sha...  53.7 us
    unnamed x1, local copies, waits for them, and re-layouts  1.32 us

profile of v3, /device:TPU:0, one launch (start us, length us, event | category | flops | bytes accessed | tf_op | source)
XLA Modules:
  0.0 55.0 jit_solution(2237577590711212211)
XLA Ops:
  0.0 53.7 %remap_step.1 = f32[32,64,256]{2,1,0:T(8,128)S(1)} custom-call(bf16[32,64,256]{2,1,0:T(8,128)(2,1)} %conc.1, s32[4,32]{1,0:T(4,128)} %bitcast.10, s32[4,32]{1,0:T(4,128)} %bitcast.11, f32[4,32]{1,0:T(4,128)} %bitcast.12, s32[1,32]{1,0:T(1,128)} %count_h.1, s32[32]{0:T(128)} %offset_h.1, f32[4,32,256]{2,1,0:T(8,128)} %rates_h.1, bf16[4,127]{1,0:T(4,128)(2,1)} %toeplitz_h.1, ...), custom_call_target="tpu_custom_call" | custom-call | tf_op jit(solution)/shard_map/remap_step/pallas_call | solution.py:409
  53.7 1.3 %copy.12 = f32[32,64,256]{2,1,0:T(8,128)} copy(f32[32,64,256]{2,1,0:T(8,128)S(1)} %remap_step.1) | data formatting | bytes 4194304

commit v4 on v3

v4 whole, which is shorter than its diff:
```python
import functools

import jax
import jax.numpy as jnp
from jax import lax
from jax.experimental import pallas as pl
from jax.experimental.pallas import tpu as pltpu
from jax.sharding import PartitionSpec as P

MESH = pl.DeviceIdType.MESH
ROWS = 32
BINS = 64
WIDTH = 256
ENTRIES = 4
GROUP = 16
GROUPS = BINS // GROUP
HALVES = 2
LANES = WIDTH // HALVES
CHUNKS = GROUPS * HALVES
BLOCK = 8
LAG = 2
TILE = 128


def kernel(
    n_lat, n_lon,
    conc, owner_h, row_h, weight_h, count_h, offset_h, rates_h, toeplitz_h, settle_h, kappa_h,
    base,
    owner_v, row_v, weight_v, count_v, offset_v, rates, toeplitz, settle, kappa,
    conc_v, taps, toep_v, stencil, places_v, mixes_v, near_places, near_mixes, places, mixes,
    fetch_sem, table_sem,
    *rest,
):
    held = rest[0:CHUNKS]
    sent = rest[CHUNKS:2 * CHUNKS]
    got = rest[2 * CHUNKS:3 * CHUNKS]
    rest = rest[3 * CHUNKS:]
    remapped, packs, halos, edges, moved = (rest[i * GROUPS:(i + 1) * GROUPS] for i in range(5))
    (dep_send, dep_recv, raw_send, raw_recv, part_send, part_recv,
     halo_send, halo_recv, edge_send, edge_recv, local_sem) = rest[5 * GROUPS:]

    lat = lax.axis_index("lat")
    lon = lax.axis_index("lon")
    core = lax.rem(lon, 2)
    chip = lon - core

    def at_lon(value):
        return lax.rem(value + 2 * n_lon, n_lon)

    sibling = chip + 1 - core
    after = at_lon(chip + 2)
    before = at_lon(chip - 1)
    beside_lon = (at_lon(lon - 1), at_lon(lon + 1))

    fetches = [
        pltpu.make_async_copy(src, dst, fetch_sem.at[i])
        for i, (src, dst) in enumerate([
            (owner_h, owner_v), (row_h, row_v), (weight_h, weight_v), (count_h, count_v), (offset_h, offset_v),
            (toeplitz_h, toeplitz), (settle_h, settle), (rates_h, rates), (kappa_h, kappa), (conc, conc_v),
        ])
    ]
    for fetch in fetches:
        fetch.start()

    def with_neighbour(side, action):
        inside = lat > 0 if side == 0 else lat < n_lat - 1
        pl.when(inside)(functools.partial(action, side, lat - 1 if side == 0 else lat + 1))

    barrier = pltpu.get_barrier_semaphore()
    for step in (-2, -1, 1, 2):
        pl.semaphore_signal(barrier, inc=1, device_id={"lon": at_lon(lon + step)}, device_id_type=MESH)

    def greet(side, there):
        pl.semaphore_signal(barrier, inc=1, device_id={"lat": there}, device_id_type=MESH)
        for across in beside_lon:
            pl.semaphore_signal(barrier, inc=1, device_id={"lat": there, "lon": across}, device_id_type=MESH)

    for side in (0, 1):
        with_neighbour(side, greet)

    for fetch in fetches[:5]:
        fetch.wait()
    owner, weight = owner_v[...], weight_v[...]
    live = lax.broadcasted_iota(jnp.int32, (ENTRIES, ROWS), 0) < count_v[...]
    places_v[...] = jnp.zeros_like(places_v)
    mixes_v[...] = jnp.zeros_like(mixes_v)
    for group, table in ((0, 0), (2, 1), (1, 2)):
        mine = live & (owner >= 5 * group) & (owner < 5 * group + 5)
        mass = jnp.where(mine, weight, 0.0)
        places_v[table, pl.ds(0, ENTRIES), :] = jnp.where(mine, (owner - 5 * group) * ROWS + row_v[...], 2 * ROWS)
        places_v[table, pl.ds(ENTRIES, 1), :] = offset_v[...]
        if group != 1:
            single = jnp.sum(mine.astype(jnp.int32), axis=0, keepdims=True) == 1
            mixes_v[2, pl.ds(ENTRIES + table, 1), :] = jnp.where(single, jnp.sum(mass, axis=0, keepdims=True), 1.0)
            mass = jnp.where(mine & single, 1.0, mass)
        mixes_v[table, pl.ds(0, ENTRIES), :] = mass
    own_tables = [
        pltpu.make_async_copy(places_v.at[2], places.at[2], table_sem.at[2, 0]),
        pltpu.make_async_copy(mixes_v.at[2], mixes.at[2], table_sem.at[2, 1]),
    ]
    for move in own_tables:
        move.start()

    def remote(src, dst, send, recv, **where):
        return pltpu.make_async_remote_copy(
            src_ref=src, dst_ref=dst, send_sem=send, recv_sem=recv, device_id=where, device_id_type=MESH
        )

    def window(c):
        g, h = c // HALVES, c % HALVES
        return conc.at[:, pl.ds(g * GROUP, GROUP), pl.ds(h * LANES, LANES)]

    def slot(c, number):
        return held[c].at[pl.ds(number * ROWS, ROWS)]

    def raw_sends(c):
        return [
            remote(window(c), slot(c, core), raw_send.at[c, 0], raw_recv.at[c, core], lon=after),
            remote(window(c), slot(c, core + 3), raw_send.at[c, 1], raw_recv.at[c, core], lon=before),
            remote(window(c), slot(c, 1 + 2 * core), raw_send.at[c, 2], raw_recv.at[c, 2], lon=sibling),
        ]

    far = 3 * core

    def raw_arrival(c, which):
        number = (far, far + 1, 3 - 2 * core, 4 - 4 * core)[which]
        return remote(window(c), slot(c, number), raw_send.at[c, 3], raw_recv.at[c, which], lon=sibling)

    def forward(c):
        return remote(
            slot(c, 1 + 2 * core), slot(c, 4 * core), raw_send.at[c, 3], raw_recv.at[c, 3], lon=sibling
        )

    def own_copy(c):
        return pltpu.make_async_copy(window(c), slot(c, 2), local_sem.at[c])

    def dep_copies(side, into, there):
        return [
            remote(places_v.at[side], near_places.at[into], dep_send.at[side, 0], dep_recv.at[into, 0], lat=there),
            remote(mixes_v.at[side], near_mixes.at[into], dep_send.at[side, 1], dep_recv.at[into, 1], lat=there),
        ]

    def dep_start(side, there):
        for copy in dep_copies(side, 1 - side, there):
            copy.start()

    pl.semaphore_wait(barrier, 4 + 3 * (jnp.where(lat > 0, 1, 0) + jnp.where(lat < n_lat - 1, 1, 0)))
    for side in (0, 1):
        with_neighbour(side, dep_start)
    for c in range(CHUNKS):
        for copy in raw_sends(c):
            copy.start()
    for c in range(CHUNKS):
        own_copy(c).start()

    for fetch in fetches[5:]:
        fetch.wait()
    toep_v[...] = jnp.zeros_like(toep_v)
    toep_v[:, pl.ds(0, 2 * BINS - 1)] = toeplitz[...].astype(jnp.float32)
    for q in range(4):
        line = jnp.broadcast_to(toep_v[pl.ds(q, 1), :], (2 * BINS, 2 * BINS))
        turned = pltpu.roll(line, BINS + 1, 1, stride=1, stride_axis=0)
        taps[pl.ds(q * BINS, BINS), :] = turned.T[:BINS, :BINS].astype(jnp.bfloat16)
    diagonal = lax.broadcasted_iota(jnp.int32, (BINS, BINS), 0) == lax.broadcasted_iota(jnp.int32, (BINS, BINS), 1)
    sinking = jnp.sum(jnp.where(diagonal, jnp.broadcast_to(settle[...], (BINS, BINS)), 0.0), axis=1, keepdims=True)
    sinking = jnp.broadcast_to(sinking, (BINS, WIDTH))

    apart = lax.broadcasted_iota(jnp.int32, (3 * TILE, WIDTH), 0) - lax.broadcasted_iota(
        jnp.int32, (3 * TILE, WIDTH), 1
    )
    near = (apart == 1) | (apart == -1) | (apart == 3 * TILE - 1)
    stencil[...] = jnp.where(near, 1.0, jnp.where(apart == 0, -4.0, 0.0)).astype(jnp.bfloat16)

    for move in own_tables:
        move.wait()

    def read_near(side, there):
        for copy in dep_copies(side, side, there):
            copy.wait_recv()
        moves = [
            pltpu.make_async_copy(near_places.at[side], places.at[side], table_sem.at[side, 0]),
            pltpu.make_async_copy(near_mixes.at[side], mixes.at[side], table_sem.at[side, 1]),
        ]
        for move in moves:
            move.start()
        for move in moves:
            move.wait()

    for side in (0, 1):
        with_neighbour(side, read_near)

    def clear(side):
        def action():
            for c in range(CHUNKS):
                got[c][side] = jnp.zeros((ROWS, GROUP, LANES), jnp.bfloat16)
            for g in range(GROUPS):
                edges[g][side] = jnp.zeros((GROUP, WIDTH), jnp.bfloat16)
                for across in (0, 1):
                    halos[g][across, 2 * side] = jnp.zeros((GROUP, TILE), jnp.bfloat16)
            places[side, ENTRIES, ROWS - 1 if side == 0 else 0] = jnp.int32(0)
        pl.when(lat == (0 if side == 0 else n_lat - 1))(action)

    for side in (0, 1):
        clear(side)

    def grow(r, _):
        cells = conc_v[r]
        product = jnp.dot(taps[...], cells, preferred_element_type=jnp.float32)
        total = -sinking * cells.astype(jnp.float32)
        for q in range(4):
            total = total + rates[q, pl.ds(r, 1), :] * product[q * BINS:(q + 1) * BINS]
        base[r] = total
        return 0

    def grow_some(c):
        share = 2 * ROWS // CHUNKS
        if c < CHUNKS // 2:
            lax.fori_loop(c * share, (c + 1) * share, grow, 0, unroll=2)

    def mixed(c, table, r):
        total = None
        for k in range(ENTRIES):
            term = mixes[table, k, r] * held[c][places[table, k, r]].astype(jnp.float32)
            total = term if total is None else total + term
        return total

    def part_copy(c, side, into, there):
        return remote(
            sent[c].at[side], got[c].at[into], part_send.at[c, side], part_recv.at[c, into], lat=there
        )

    def partials(c):
        def action(side, there):
            def one(r, _):
                sent[c][side, r] = mixed(c, side, r).astype(jnp.bfloat16)
                return 0
            lax.fori_loop(0, ROWS, one, 0, unroll=4)
            part_copy(c, side, 1 - side, there).start()
        for side in (0, 1):
            with_neighbour(side, action)

    lane = lax.broadcasted_iota(jnp.int32, (GROUP, TILE), 1)

    def wanted(step):
        return jnp.where(step > -1, step + 1, 0), jnp.where(step < 1, 1 - step, 0)

    def remap(c):
        g, h = c // HALVES, c % HALVES
        for side in (0, 1):
            with_neighbour(side, lambda side, there: part_copy(c, side, side, there).wait_recv())
        sides = {0: [0], 1: [1]}[h] if HALVES == 2 else [0, 1]

        def one(r, packed):
            total = mixed(c, 2, r)
            for side in (0, 1):
                total = total + mixes[2, ENTRIES + side, r] * got[c][side, r].astype(jnp.float32)
            rounded = total.astype(jnp.bfloat16)
            remapped[g][r, :, pl.ds(h * LANES, LANES)] = rounded
            rounded = rounded.astype(jnp.float32)
            before_row, after_row = wanted(places[2, ENTRIES, r])
            start = 4 * r + before_row
            found = []
            for side, kept in zip(sides, packed):
                tile = rounded[:, :TILE] if side == 0 else rounded[:, LANES - TILE:]
                if side == 0:
                    here = (lane >= start) & (lane < start + after_row)
                else:
                    here = (lane >= 4 * r) & (lane < start)
                found.append(jnp.where(here, pltpu.roll(tile, lax.rem(start, TILE), 1), kept))
            return tuple(found)

        empty = jnp.zeros((GROUP, TILE), jnp.float32)
        packed = lax.fori_loop(0, ROWS, one, (empty,) * len(sides), unroll=4)
        for side, tile in zip(sides, packed):
            packs[g][side] = tile.astype(jnp.bfloat16)

    def halo_copy(g, across, up, into_across, into_up, where):
        return remote(
            packs[g].at[across], halos[g].at[into_across, into_up],
            halo_send.at[g, across, up], halo_recv.at[g, into_across, into_up], **where
        )

    def edge_copy(g, side, into, there):
        row = 0 if side == 0 else ROWS - 1
        return remote(
            remapped[g].at[row], edges[g].at[into], edge_send.at[g, side], edge_recv.at[g, into], lat=there
        )

    def outgoing(g, act):
        for across in (0, 1):
            act(halo_copy(g, across, 1, 1 - across, 1, {"lon": beside_lon[across]}))

        def action(side, there):
            act(edge_copy(g, side, 1 - side, there))
            for across in (0, 1):
                act(halo_copy(
                    g, across, 2 * side, 1 - across, 2 - 2 * side, {"lat": there, "lon": beside_lon[across]}
                ))

        for side in (0, 1):
            with_neighbour(side, action)

    def incoming(g):
        for across in (0, 1):
            halo_copy(g, across, 1, across, 1, {"lon": beside_lon[across]}).wait_recv()

        def action(side, there):
            edge_copy(g, side, side, there).wait_recv()
            for across in (0, 1):
                halo_copy(
                    g, across, 2 * side, across, 2 * side, {"lat": there, "lon": beside_lon[across]}
                ).wait_recv()

        for side in (0, 1):
            with_neighbour(side, action)

    def shifted(line, packed, r, step):
        left, right = line[:, :TILE], line[:, TILE:]
        turn = jnp.where(step < 0, step + TILE, step)
        low, high = lane < step, lane >= TILE + step
        halo = pltpu.roll(packed, lax.rem(turn + 2 * TILE - 4 * r - wanted(step)[0], TILE), 1)
        left, right = pltpu.roll(left, turn, 1), pltpu.roll(right, turn, 1)

        def pick(prior, tile, later):
            return jnp.where(low, prior, jnp.where(high, later, tile))

        tiles = pick(halo, left, right), pick(left, right, halo), pick(right, halo, left)
        return jnp.concatenate(tiles, axis=1).astype(jnp.bfloat16)

    def finish(g):
        incoming(g)

        def packed(up):
            return halos[g][0, up].astype(jnp.float32) + halos[g][1, up].astype(jnp.float32)

        middle = packed(1)

        def shift(r, _):
            moved[g][r + 1] = shifted(remapped[g][r].astype(jnp.float32), middle, r, places[2, ENTRIES, r])
            return 0

        lax.fori_loop(0, ROWS, shift, 0, unroll=4)
        for side in (0, 1):
            r = ROWS - 1 if side == 0 else 0
            moved[g][(ROWS + 1) * side] = shifted(
                edges[g][side].astype(jnp.float32), packed(2 * side), jnp.int32(r), places[side, ENTRIES, r]
            )
        bins = pl.ds(g * GROUP, GROUP)

        def block(n, _):
            first = n * BLOCK
            lines = moved[g][pl.ds(first + 1, BLOCK)].reshape(BLOCK * GROUP, 3 * TILE)
            along = jnp.dot(lines, stencil[...], preferred_element_type=jnp.float32)
            for i in range(BLOCK):
                r = first + i
                center, above, below = (
                    moved[g][r + d, :, pl.ds(0, WIDTH)].astype(jnp.float32) for d in (1, 0, 2)
                )
                total = base[r, bins, :] + center
                base[r, bins, :] = total + kappa[pl.ds(r, 1), :] * (
                    (above + below) + along[i * GROUP:(i + 1) * GROUP]
                )
            return 0

        lax.fori_loop(0, ROWS // BLOCK, block, 0)

    def settle_chunk(c):
        remap(c)
        if c % HALVES == HALVES - 1:
            outgoing(c // HALVES, lambda copy: copy.start())

    for c in range(CHUNKS):
        for which in (0, 1):
            raw_arrival(c, which).wait_recv()
        forward(c).start()
        grow_some(c)
        own_copy(c).wait()
        for which in (2, 3):
            raw_arrival(c, which).wait_recv()
        partials(c)
        if c >= LAG:
            settle_chunk(c - LAG)
    finished = 0
    for c in range(CHUNKS - LAG, CHUNKS):
        settle_chunk(c)
        if finished < (c - 1) // HALVES:
            finish(finished)
            finished += 1
    for g in range(finished, GROUPS):
        finish(g)

    for c in range(CHUNKS):
        for copy in raw_sends(c):
            copy.wait_send()
        forward(c).wait_send()
        for side in (0, 1):
            with_neighbour(side, lambda side, there: part_copy(c, side, 1 - side, there).wait_send())
    for g in range(GROUPS):
        outgoing(g, lambda copy: copy.wait_send())

    def dep_sent(side, there):
        for copy in dep_copies(side, 1 - side, there):
            copy.wait_send()

    for side in (0, 1):
        with_neighbour(side, dep_sent)


def solution(mesh):
    n_lat, n_lon = mesh.shape["lat"], mesh.shape["lon"]

    def body(conc, dep_owner, dep_row, dep_weight, dep_count, zonal_offset, agg_rates, toeplitz, settle, kappa):
        owner, row, weight = dep_owner[0].T, dep_row[0].T, dep_weight[0].T
        hbm = pl.BlockSpec(memory_space=pltpu.HBM)
        bf16, f32, i32 = jnp.bfloat16, jnp.float32, jnp.int32
        dma = pltpu.SemaphoreType.DMA
        return pl.pallas_call(
            functools.partial(kernel, n_lat, n_lon),
            out_shape=jax.ShapeDtypeStruct((ROWS, BINS, WIDTH), f32),
            in_specs=[hbm] * 10,
            out_specs=pl.BlockSpec(memory_space=pltpu.VMEM),
            scratch_shapes=[
                pltpu.VMEM((ENTRIES, ROWS), i32),
                pltpu.VMEM((ENTRIES, ROWS), i32),
                pltpu.VMEM((ENTRIES, ROWS), f32),
                pltpu.VMEM((1, ROWS), i32),
                pltpu.VMEM((1, ROWS), i32),
                pltpu.VMEM((4, ROWS, WIDTH), f32),
                pltpu.VMEM((4, 2 * BINS - 1), bf16),
                pltpu.VMEM((1, BINS), f32),
                pltpu.VMEM((ROWS, WIDTH), f32),
                pltpu.VMEM((ROWS, BINS, WIDTH), bf16),
                pltpu.VMEM((4 * BINS, BINS), bf16),
                pltpu.VMEM((4, 2 * BINS), f32),
                pltpu.VMEM((3 * TILE, WIDTH), bf16),
                pltpu.VMEM((3, 8, ROWS), i32),
                pltpu.VMEM((3, 8, ROWS), f32),
                pltpu.VMEM((2, 8, ROWS), i32),
                pltpu.VMEM((2, 8, ROWS), f32),
                pltpu.SMEM((3, 8, ROWS), i32),
                pltpu.SMEM((3, 8, ROWS), f32),
                dma((10,)),
                dma((3, 2)),
            ]
            + [pltpu.VMEM((5 * ROWS, GROUP, LANES), bf16) for _ in range(CHUNKS)]
            + [pltpu.VMEM((2, ROWS, GROUP, LANES), bf16) for _ in range(2 * CHUNKS)]
            + [pltpu.VMEM((ROWS, GROUP, WIDTH), bf16) for _ in range(GROUPS)]
            + [pltpu.VMEM((2, GROUP, TILE), bf16) for _ in range(GROUPS)]
            + [pltpu.VMEM((2, 3, GROUP, TILE), bf16) for _ in range(GROUPS)]
            + [pltpu.VMEM((2, GROUP, WIDTH), bf16) for _ in range(GROUPS)]
            + [pltpu.VMEM((ROWS + 2, GROUP, 3 * TILE), bf16) for _ in range(GROUPS)]
            + [
                dma((2, 2)), dma((2, 2)),
                dma((CHUNKS, 4)), dma((CHUNKS, 4)),
                dma((CHUNKS, 2)), dma((CHUNKS, 2)),
                dma((GROUPS, 2, 3)), dma((GROUPS, 2, 3)),
                dma((GROUPS, 2)), dma((GROUPS, 2)),
                dma((CHUNKS,)),
            ],
            compiler_params=pltpu.CompilerParams(
                collective_id=0, has_side_effects=True, vmem_limit_bytes=40 << 20
            ),
            name="remap_step",
        )(
            *[
                pltpu.with_memory_space_constraint(operand, pltpu.HBM)
                for operand in (
                    conc, owner, row, weight, dep_count, zonal_offset.reshape(1, ROWS), agg_rates, toeplitz,
                    settle.reshape(1, BINS), kappa,
                )
            ]
        )

    return jax.shard_map(
        body,
        mesh=mesh,
        in_specs=(
            P("lat", None, "lon"),
            P("lon", "lat", None),
            P("lon", "lat", None),
            P("lon", "lat", None),
            P("lon", "lat"),
            P("lat"),
            P(None, "lat", "lon"),
            P(),
            P(),
            P("lat", "lon"),
        ),
        out_specs=P("lat", None, "lon"),
        check_vma=False,
    )
```

time: 55.1 us -> 50.9 us (0.924)
  Pallas kernels: 53.7 us -> 49.4 us
    pallas_call x1, Pallas kernels: 53.7 us -> 49.4 us  [body(): pl.pallas_call(functools.partial(kernel, n_lat, n_lon), out_shape=jax.Sha...]
where the time goes in v4:
time: 50.9 us; the launch traced here: 50.7 us
  Pallas kernels  49.4 us (97%)
  local copies, waits for them, and re-layouts  1.32 us (3%)
    pallas_call x1, Pallas kernels, body(): pl.pallas_call(functools.partial(kernel, n_lat, n_lon), out_shape=jax.Sha...  49.4 us
    unnamed x1, local copies, waits for them, and re-layouts  1.32 us

profile of v4, /device:TPU:0, one launch (start us, length us, event | category | flops | bytes accessed | tf_op | source)
XLA Modules:
  0.0 50.7 jit_solution(16357927169416126591)
XLA Ops:
  0.0 49.4 %remap_step.1 = f32[32,64,256]{2,1,0:T(8,128)S(1)} custom-call(bf16[32,64,256]{2,1,0:T(8,128)(2,1)} %conc.1, s32[4,32]{1,0:T(4,128)} %bitcast.11, s32[4,32]{1,0:T(4,128)} %bitcast.12, f32[4,32]{1,0:T(4,128)} %bitcast.13, s32[1,32]{1,0:T(1,128)} %count_h.1, s32[1,32]{1,0:T(1,128)} %bitcast.14, f32[4,32,256]{2,1,0:T(8,128)} %rates_h.1, ...), custom_call_target="tpu_custom_call" | custom-call | tf_op jit(solution)/shard_map/remap_step/pallas_call | solution.py:417
  49.4 1.3 %copy.12 = f32[32,64,256]{2,1,0:T(8,128)} copy(f32[32,64,256]{2,1,0:T(8,128)S(1)} %remap_step.1) | data formatting | bytes 4194304

commit v5 on v4

--- a/solution.py
+++ b/solution.py
@@ -17,8 +17,8 @@
 HALVES = 2
 LANES = WIDTH // HALVES
 CHUNKS = GROUPS * HALVES
-BLOCK = 8
-LAG = 2
+BLOCK = 16
+LAG = 3
 TILE = 128
 
 
@@ -35,9 +35,11 @@
     sent = rest[CHUNKS:2 * CHUNKS]
     got = rest[2 * CHUNKS:3 * CHUNKS]
     rest = rest[3 * CHUNKS:]
-    remapped, packs, halos, edges, moved = (rest[i * GROUPS:(i + 1) * GROUPS] for i in range(5))
+    remapped, packs, halos, corners, edges, moved = (
+        rest[i * GROUPS:(i + 1) * GROUPS] for i in range(6)
+    )
     (dep_send, dep_recv, raw_send, raw_recv, part_send, part_recv,
-     halo_send, halo_recv, edge_send, edge_recv, local_sem) = rest[5 * GROUPS:]
+     halo_send, halo_recv, corner_send, corner_recv, edge_send, edge_recv, local_sem) = rest[6 * GROUPS:]
 
     lat = lax.axis_index("lat")
     lon = lax.axis_index("lon")
@@ -51,6 +53,22 @@
     after = at_lon(chip + 2)
     before = at_lon(chip - 1)
     beside_lon = (at_lon(lon - 1), at_lon(lon + 1))
+
+    def with_neighbour(side, action):
+        inside = lat > 0 if side == 0 else lat < n_lat - 1
+        pl.when(inside)(functools.partial(action, side, lat - 1 if side == 0 else lat + 1))
+
+    barrier = pltpu.get_barrier_semaphore()
+    for step in (-2, -1, 1, 2):
+        pl.semaphore_signal(barrier, inc=1, device_id={"lon": at_lon(lon + step)}, device_id_type=MESH)
+
+    def greet(side, there):
+        pl.semaphore_signal(barrier, inc=1, device_id={"lat": there}, device_id_type=MESH)
+        for across in beside_lon:
+            pl.semaphore_signal(barrier, inc=1, device_id={"lat": there, "lon": across}, device_id_type=MESH)
+
+    for side in (0, 1):
+        with_neighbour(side, greet)
 
     fetches = [
         pltpu.make_async_copy(src, dst, fetch_sem.at[i])
@@ -62,21 +80,55 @@
     for fetch in fetches:
         fetch.start()
 
-    def with_neighbour(side, action):
-        inside = lat > 0 if side == 0 else lat < n_lat - 1
-        pl.when(inside)(functools.partial(action, side, lat - 1 if side == 0 else lat + 1))
-
-    barrier = pltpu.get_barrier_semaphore()
-    for step in (-2, -1, 1, 2):
-        pl.semaphore_signal(barrier, inc=1, device_id={"lon": at_lon(lon + step)}, device_id_type=MESH)
-
-    def greet(side, there):
-        pl.semaphore_signal(barrier, inc=1, device_id={"lat": there}, device_id_type=MESH)
-        for across in beside_lon:
-            pl.semaphore_signal(barrier, inc=1, device_id={"lat": there, "lon": across}, device_id_type=MESH)
-
-    for side in (0, 1):
-        with_neighbour(side, greet)
+    def remote(src, dst, send, recv, **where):
+        return pltpu.make_async_remote_copy(
+            src_ref=src, dst_ref=dst, send_sem=send, recv_sem=recv, device_id=where, device_id_type=MESH
+        )
+
+    def window(c):
+        g, h = c // HALVES, c % HALVES
+        return conc.at[:, pl.ds(g * GROUP, GROUP), pl.ds(h * LANES, LANES)]
+
+    def slot(c, number):
+        return held[c].at[pl.ds(number * ROWS, ROWS)]
+
+    def raw_sends(c):
+        return [
+            remote(window(c), slot(c, core), raw_send.at[c, 0], raw_recv.at[c, core], lon=after),
+            remote(window(c), slot(c, core + 3), raw_send.at[c, 1], raw_recv.at[c, core], lon=before),
+            remote(window(c), slot(c, 1 + 2 * core), raw_send.at[c, 2], raw_recv.at[c, 2], lon=sibling),
+        ]
+
+    far = 3 * core
+
+    def raw_arrival(c, which):
+        number = (far, far + 1, 3 - 2 * core, 4 - 4 * core)[which]
+        return remote(window(c), slot(c, number), raw_send.at[c, 3], raw_recv.at[c, which], lon=sibling)
+
+    def forward(c):
+        return remote(
+            slot(c, 1 + 2 * core), slot(c, 4 * core), raw_send.at[c, 3], raw_recv.at[c, 3], lon=sibling
+        )
+
+    def own_copy(c):
+        return pltpu.make_async_copy(window(c), slot(c, 2), local_sem.at[c])
+
+    def dep_copies(side, into, there):
+        return [
+            remote(places_v.at[side], near_places.at[into], dep_send.at[side, 0], dep_recv.at[into, 0], lat=there),
+            remote(mixes_v.at[side], near_mixes.at[into], dep_send.at[side, 1], dep_recv.at[into, 1], lat=there),
+        ]
+
+    def dep_start(side, there):
+        for copy in dep_copies(side, 1 - side, there):
+            copy.start()
+
+    pl.semaphore_wait(barrier, 4 + 3 * (jnp.where(lat > 0, 1, 0) + jnp.where(lat < n_lat - 1, 1, 0)))
+    for c in range(CHUNKS):
+        for copy in raw_sends(c):
+            copy.start()
+    for c in range(CHUNKS):
+        own_copy(c).start()
 
     for fetch in fetches[:5]:
         fetch.wait()
@@ -101,58 +153,8 @@
     for move in own_tables:
         move.start()
 
-    def remote(src, dst, send, recv, **where):
-        return pltpu.make_async_remote_copy(
-            src_ref=src, dst_ref=dst, send_sem=send, recv_sem=recv, device_id=where, device_id_type=MESH
-        )
-
-    def window(c):
-        g, h = c // HALVES, c % HALVES
-        return conc.at[:, pl.ds(g * GROUP, GROUP), pl.ds(h * LANES, LANES)]
-
-    def slot(c, number):
-        return held[c].at[pl.ds(number * ROWS, ROWS)]
-
-    def raw_sends(c):
-        return [
-            remote(window(c), slot(c, core), raw_send.at[c, 0], raw_recv.at[c, core], lon=after),
-            remote(window(c), slot(c, core + 3), raw_send.at[c, 1], raw_recv.at[c, core], lon=before),
-            remote(window(c), slot(c, 1 + 2 * core), raw_send.at[c, 2], raw_recv.at[c, 2], lon=sibling),
-        ]
-
-    far = 3 * core
-
-    def raw_arrival(c, which):
-        number = (far, far + 1, 3 - 2 * core, 4 - 4 * core)[which]
-        return remote(window(c), slot(c, number), raw_send.at[c, 3], raw_recv.at[c, which], lon=sibling)
-
-    def forward(c):
-        return remote(
-            slot(c, 1 + 2 * core), slot(c, 4 * core), raw_send.at[c, 3], raw_recv.at[c, 3], lon=sibling
-        )
-
-    def own_copy(c):
-        return pltpu.make_async_copy(window(c), slot(c, 2), local_sem.at[c])
-
-    def dep_copies(side, into, there):
-        return [
-            remote(places_v.at[side], near_places.at[into], dep_send.at[side, 0], dep_recv.at[into, 0], lat=there),
-            remote(mixes_v.at[side], near_mixes.at[into], dep_send.at[side, 1], dep_recv.at[into, 1], lat=there),
-        ]
-
-    def dep_start(side, there):
-        for copy in dep_copies(side, 1 - side, there):
-            copy.start()
-
-    pl.semaphore_wait(barrier, 4 + 3 * (jnp.where(lat > 0, 1, 0) + jnp.where(lat < n_lat - 1, 1, 0)))
     for side in (0, 1):
         with_neighbour(side, dep_start)
-    for c in range(CHUNKS):
-        for copy in raw_sends(c):
-            copy.start()
-    for c in range(CHUNKS):
-        own_copy(c).start()
-
     for fetch in fetches[5:]:
         fetch.wait()
     toep_v[...] = jnp.zeros_like(toep_v)
@@ -195,8 +197,7 @@
                 got[c][side] = jnp.zeros((ROWS, GROUP, LANES), jnp.bfloat16)
             for g in range(GROUPS):
                 edges[g][side] = jnp.zeros((GROUP, WIDTH), jnp.bfloat16)
-                for across in (0, 1):
-                    halos[g][across, 2 * side] = jnp.zeros((GROUP, TILE), jnp.bfloat16)
+                corners[g][side] = jnp.zeros((2, GROUP, TILE), jnp.bfloat16)
             places[side, ENTRIES, ROWS - 1 if side == 0 else 0] = jnp.int32(0)
         pl.when(lat == (0 if side == 0 else n_lat - 1))(action)
 
@@ -234,7 +235,7 @@
             def one(r, _):
                 sent[c][side, r] = mixed(c, side, r).astype(jnp.bfloat16)
                 return 0
-            lax.fori_loop(0, ROWS, one, 0, unroll=4)
+            lax.fori_loop(0, ROWS, one, 0, unroll=16)
             part_copy(c, side, 1 - side, there).start()
         for side in (0, 1):
             with_neighbour(side, action)
@@ -248,36 +249,41 @@
         g, h = c // HALVES, c % HALVES
         for side in (0, 1):
             with_neighbour(side, lambda side, there: part_copy(c, side, side, there).wait_recv())
-        sides = {0: [0], 1: [1]}[h] if HALVES == 2 else [0, 1]
-
-        def one(r, packed):
+
+        def one(r, _):
             total = mixed(c, 2, r)
             for side in (0, 1):
                 total = total + mixes[2, ENTRIES + side, r] * got[c][side, r].astype(jnp.float32)
-            rounded = total.astype(jnp.bfloat16)
-            remapped[g][r, :, pl.ds(h * LANES, LANES)] = rounded
-            rounded = rounded.astype(jnp.float32)
+            remapped[g][r, :, pl.ds(h * LANES, LANES)] = total.astype(jnp.bfloat16)
+            return 0
+
+        one(0, 0)
+        one(ROWS - 1, 0)
+        if h == HALVES - 1:
+            outer_sends(g, lambda copy: copy.start())
+        lax.fori_loop(1, ROWS - 1, one, 0, unroll=10)
+
+    def pack(g):
+        first_cells = jnp.zeros((GROUP, TILE), jnp.float32)
+        last_cells = first_cells
+        for r in range(ROWS):
             before_row, after_row = wanted(places[2, ENTRIES, r])
             start = 4 * r + before_row
-            found = []
-            for side, kept in zip(sides, packed):
-                tile = rounded[:, :TILE] if side == 0 else rounded[:, LANES - TILE:]
-                if side == 0:
-                    here = (lane >= start) & (lane < start + after_row)
-                else:
-                    here = (lane >= 4 * r) & (lane < start)
-                found.append(jnp.where(here, pltpu.roll(tile, lax.rem(start, TILE), 1), kept))
-            return tuple(found)
-
-        empty = jnp.zeros((GROUP, TILE), jnp.float32)
-        packed = lax.fori_loop(0, ROWS, one, (empty,) * len(sides), unroll=4)
-        for side, tile in zip(sides, packed):
-            packs[g][side] = tile.astype(jnp.bfloat16)
-
-    def halo_copy(g, across, up, into_across, into_up, where):
+            turn = jnp.where(start < TILE, start, 0)
+            line = remapped[g][r].astype(jnp.float32)
+            first_cells = jnp.where(
+                (lane >= start) & (lane < start + after_row), pltpu.roll(line[:, :TILE], turn, 1), first_cells
+            )
+            last_cells = jnp.where(
+                (lane >= 4 * r) & (lane < start), pltpu.roll(line[:, TILE:], turn, 1), last_cells
+            )
+        packs[g][0] = first_cells.astype(jnp.bfloat16)
+        packs[g][1] = last_cells.astype(jnp.bfloat16)
+
+    def halo_copy(g, across, into_across, where):
         return remote(
-            packs[g].at[across], halos[g].at[into_across, into_up],
-            halo_send.at[g, across, up], halo_recv.at[g, into_across, into_up], **where
+            packs[g].at[across], halos[g].at[into_across],
+            halo_send.at[g, across], halo_recv.at[g, into_across], **where
         )
 
     def edge_copy(g, side, into, there):
@@ -286,39 +292,46 @@
             remapped[g].at[row], edges[g].at[into], edge_send.at[g, side], edge_recv.at[g, into], lat=there
         )
 
-    def outgoing(g, act):
-        for across in (0, 1):
-            act(halo_copy(g, across, 1, 1 - across, 1, {"lon": beside_lon[across]}))
-
+    def corner_copy(g, side, across, into, into_across, where):
+        row, first_lane = (0 if side == 0 else ROWS - 1), (0 if across == 0 else WIDTH - TILE)
+        return remote(
+            remapped[g].at[row, :, pl.ds(first_lane, TILE)], corners[g].at[into, into_across],
+            corner_send.at[g, side, across], corner_recv.at[g, into, into_across], **where
+        )
+
+    def outer_sends(g, act):
         def action(side, there):
             act(edge_copy(g, side, 1 - side, there))
             for across in (0, 1):
-                act(halo_copy(
-                    g, across, 2 * side, 1 - across, 2 - 2 * side, {"lat": there, "lon": beside_lon[across]}
+                act(corner_copy(
+                    g, side, across, 1 - side, 1 - across, {"lat": there, "lon": beside_lon[across]}
                 ))
 
         for side in (0, 1):
             with_neighbour(side, action)
 
+    def outgoing(g, act):
+        for across in (0, 1):
+            act(halo_copy(g, across, 1 - across, {"lon": beside_lon[across]}))
+
     def incoming(g):
-        for across in (0, 1):
-            halo_copy(g, across, 1, across, 1, {"lon": beside_lon[across]}).wait_recv()
-
         def action(side, there):
             edge_copy(g, side, side, there).wait_recv()
             for across in (0, 1):
-                halo_copy(
-                    g, across, 2 * side, across, 2 * side, {"lat": there, "lon": beside_lon[across]}
+                corner_copy(
+                    g, side, across, side, across, {"lat": there, "lon": beside_lon[across]}
                 ).wait_recv()
 
         for side in (0, 1):
             with_neighbour(side, action)
-
-    def shifted(line, packed, r, step):
+        for across in (0, 1):
+            halo_copy(g, across, across, {"lon": beside_lon[across]}).wait_recv()
+
+    def shifted(line, halo, turned, step):
         left, right = line[:, :TILE], line[:, TILE:]
         turn = jnp.where(step < 0, step + TILE, step)
         low, high = lane < step, lane >= TILE + step
-        halo = pltpu.roll(packed, lax.rem(turn + 2 * TILE - 4 * r - wanted(step)[0], TILE), 1)
+        halo = pltpu.roll(halo, lax.rem(turn + 2 * TILE - turned, TILE), 1)
         left, right = pltpu.roll(left, turn, 1), pltpu.roll(right, turn, 1)
 
         def pick(prior, tile, later):
@@ -330,21 +343,19 @@
     def finish(g):
         incoming(g)
 
-        def packed(up):
-            return halos[g][0, up].astype(jnp.float32) + halos[g][1, up].astype(jnp.float32)
-
-        middle = packed(1)
+        middle = halos[g][0].astype(jnp.float32) + halos[g][1].astype(jnp.float32)
+
+        for side in (0, 1):
+            halo = jnp.where(lane < TILE // 2, corners[g][side, 1], corners[g][side, 0]).astype(jnp.float32)
+            step = places[side, ENTRIES, ROWS - 1 if side == 0 else 0]
+            moved[g][(ROWS + 1) * side] = shifted(edges[g][side].astype(jnp.float32), halo, jnp.int32(0), step)
 
         def shift(r, _):
-            moved[g][r + 1] = shifted(remapped[g][r].astype(jnp.float32), middle, r, places[2, ENTRIES, r])
+            step = places[2, ENTRIES, r]
+            moved[g][r + 1] = shifted(remapped[g][r].astype(jnp.float32), middle, 4 * r + wanted(step)[0], step)
             return 0
 
-        lax.fori_loop(0, ROWS, shift, 0, unroll=4)
-        for side in (0, 1):
-            r = ROWS - 1 if side == 0 else 0
-            moved[g][(ROWS + 1) * side] = shifted(
-                edges[g][side].astype(jnp.float32), packed(2 * side), jnp.int32(r), places[side, ENTRIES, r]
-            )
+        lax.fori_loop(0, ROWS, shift, 0, unroll=16)
         bins = pl.ds(g * GROUP, GROUP)
 
         def block(n, _):
@@ -367,6 +378,7 @@
     def settle_chunk(c):
         remap(c)
         if c % HALVES == HALVES - 1:
+            pack(c // HALVES)
             outgoing(c // HALVES, lambda copy: copy.start())
 
     for c in range(CHUNKS):
@@ -374,16 +386,16 @@
             raw_arrival(c, which).wait_recv()
         forward(c).start()
         grow_some(c)
+        if c >= LAG:
+            settle_chunk(c - LAG)
         own_copy(c).wait()
         for which in (2, 3):
             raw_arrival(c, which).wait_recv()
         partials(c)
-        if c >= LAG:
-            settle_chunk(c - LAG)
     finished = 0
     for c in range(CHUNKS - LAG, CHUNKS):
         settle_chunk(c)
-        if finished < (c - 1) // HALVES:
+        if c < CHUNKS - 1:
             finish(finished)
             finished += 1
     for g in range(finished, GROUPS):
@@ -397,6 +409,7 @@
             with_neighbour(side, lambda side, there: part_copy(c, side, 1 - side, there).wait_send())
     for g in range(GROUPS):
         outgoing(g, lambda copy: copy.wait_send())
+        outer_sends(g, lambda copy: copy.wait_send())
 
     def dep_sent(side, there):
         for copy in dep_copies(side, 1 - side, there):
@@ -446,14 +459,16 @@
             + [pltpu.VMEM((2, ROWS, GROUP, LANES), bf16) for _ in range(2 * CHUNKS)]
             + [pltpu.VMEM((ROWS, GROUP, WIDTH), bf16) for _ in range(GROUPS)]
             + [pltpu.VMEM((2, GROUP, TILE), bf16) for _ in range(GROUPS)]
-            + [pltpu.VMEM((2, 3, GROUP, TILE), bf16) for _ in range(GROUPS)]
+            + [pltpu.VMEM((2, GROUP, TILE), bf16) for _ in range(GROUPS)]
+            + [pltpu.VMEM((2, 2, GROUP, TILE), bf16) for _ in range(GROUPS)]
             + [pltpu.VMEM((2, GROUP, WIDTH), bf16) for _ in range(GROUPS)]
             + [pltpu.VMEM((ROWS + 2, GROUP, 3 * TILE), bf16) for _ in range(GROUPS)]
             + [
                 dma((2, 2)), dma((2, 2)),
                 dma((CHUNKS, 4)), dma((CHUNKS, 4)),
                 dma((CHUNKS, 2)), dma((CHUNKS, 2)),
-                dma((GROUPS, 2, 3)), dma((GROUPS, 2, 3)),
+                dma((GROUPS, 2)), dma((GROUPS, 2)),
+                dma((GROUPS, 2, 2)), dma((GROUPS, 2, 2)),
                 dma((GROUPS, 2)), dma((GROUPS, 2)),
                 dma((CHUNKS,)),
             ],

time: 50.9 us -> 49.2 us (0.967)
  Pallas kernels: 49.4 us -> 47.7 us
    pallas_call x1, Pallas kernels: 49.4 us -> 47.7 us  [body(): pl.pallas_call(functools.partial(kernel, n_lat, n_lon), out_shape=jax.Sha...]
where the time goes in v5:
time: 49.2 us; the launch traced here: 49.1 us
  Pallas kernels  47.7 us (97%)
  local copies, waits for them, and re-layouts  1.32 us (3%)
    pallas_call x1, Pallas kernels, body(): pl.pallas_call(functools.partial(kernel, n_lat, n_lon), out_shape=jax.Sha...  47.7 us
    unnamed x1, local copies, waits for them, and re-layouts  1.32 us

profile of v5, /device:TPU:0, one launch (start us, length us, event | category | flops | bytes accessed | tf_op | source)
XLA Modules:
  0.0 49.1 jit_solution(12069859306027760246)
XLA Ops:
  0.0 47.7 %remap_step.1 = f32[32,64,256]{2,1,0:T(8,128)S(1)} custom-call(bf16[32,64,256]{2,1,0:T(8,128)(2,1)} %conc.1, s32[4,32]{1,0:T(4,128)} %bitcast.11, s32[4,32]{1,0:T(4,128)} %bitcast.12, f32[4,32]{1,0:T(4,128)} %bitcast.13, s32[1,32]{1,0:T(1,128)} %count_h.1, s32[1,32]{1,0:T(1,128)} %bitcast.14, f32[4,32,256]{2,1,0:T(8,128)} %rates_h.1, ...), custom_call_target="tpu_custom_call" | custom-call | tf_op jit(solution)/shard_map/remap_step/pallas_call | solution.py:430
  47.8 1.3 %copy.12 = f32[32,64,256]{2,1,0:T(8,128)} copy(f32[32,64,256]{2,1,0:T(8,128)S(1)} %remap_step.1) | data formatting | bytes 4194304

commit v6 on v5

--- a/solution.py
+++ b/solution.py
@@ -18,6 +18,7 @@
 LANES = WIDTH // HALVES
 CHUNKS = GROUPS * HALVES
 BLOCK = 16
+AHEAD = 2
 LAG = 3
 TILE = 128
 
@@ -92,18 +93,21 @@
     def slot(c, number):
         return held[c].at[pl.ds(number * ROWS, ROWS)]
 
-    def raw_sends(c):
-        return [
-            remote(window(c), slot(c, core), raw_send.at[c, 0], raw_recv.at[c, core], lon=after),
-            remote(window(c), slot(c, core + 3), raw_send.at[c, 1], raw_recv.at[c, core], lon=before),
-            remote(window(c), slot(c, 1 + 2 * core), raw_send.at[c, 2], raw_recv.at[c, 2], lon=sibling),
-        ]
-
-    far = 3 * core
-
-    def raw_arrival(c, which):
-        number = (far, far + 1, 3 - 2 * core, 4 - 4 * core)[which]
-        return remote(window(c), slot(c, number), raw_send.at[c, 3], raw_recv.at[c, which], lon=sibling)
+    single_to = jnp.where(core == 0, after, before)
+    double_to = jnp.where(core == 0, before, after)
+
+    def single_send(c):
+        return remote(window(c), slot(c, 4 * core), raw_send.at[c, 0], raw_recv.at[c, 0], lon=single_to)
+
+    def double_send(c):
+        return remote(window(c), slot(c, 3 - 2 * core), raw_send.at[c, 1], raw_recv.at[c, 1], lon=double_to)
+
+    def sibling_send(c):
+        return remote(window(c), slot(c, 1 + 2 * core), raw_send.at[c, 2], raw_recv.at[c, 2], lon=sibling)
+
+    def raw_arrival(c, kind):
+        number = (4 * core, 1 + 2 * core, 3 - 2 * core, 4 - 4 * core)[kind]
+        return remote(window(c), slot(c, number), raw_send.at[c, 3], raw_recv.at[c, kind], lon=sibling)
 
     def forward(c):
         return remote(
@@ -125,8 +129,10 @@
 
     pl.semaphore_wait(barrier, 4 + 3 * (jnp.where(lat > 0, 1, 0) + jnp.where(lat < n_lat - 1, 1, 0)))
     for c in range(CHUNKS):
-        for copy in raw_sends(c):
-            copy.start()
+        double_send(c).start()
+        if c < AHEAD:
+            single_send(c).start()
+        sibling_send(c).start()
     for c in range(CHUNKS):
         own_copy(c).start()
 
@@ -216,7 +222,7 @@
     def grow_some(c):
         share = 2 * ROWS // CHUNKS
         if c < CHUNKS // 2:
-            lax.fori_loop(c * share, (c + 1) * share, grow, 0, unroll=2)
+            lax.fori_loop(c * share, (c + 1) * share, grow, 0, unroll=8)
 
     def mixed(c, table, r):
         total = None
@@ -382,27 +388,27 @@
             outgoing(c // HALVES, lambda copy: copy.start())
 
     for c in range(CHUNKS):
-        for which in (0, 1):
-            raw_arrival(c, which).wait_recv()
+        raw_arrival(c, 1).wait_recv()
         forward(c).start()
         grow_some(c)
         if c >= LAG:
             settle_chunk(c - LAG)
         own_copy(c).wait()
-        for which in (2, 3):
-            raw_arrival(c, which).wait_recv()
+        raw_arrival(c, 0).wait_recv()
+        if c + AHEAD < CHUNKS:
+            single_send(c + AHEAD).start()
+        for kind in (2, 3):
+            raw_arrival(c, kind).wait_recv()
         partials(c)
-    finished = 0
     for c in range(CHUNKS - LAG, CHUNKS):
         settle_chunk(c)
-        if c < CHUNKS - 1:
-            finish(finished)
-            finished += 1
-    for g in range(finished, GROUPS):
+        if c == CHUNKS - 2:
+            finish(0)
+    for g in range(1, GROUPS):
         finish(g)
 
     for c in range(CHUNKS):
-        for copy in raw_sends(c):
+        for copy in (single_send(c), double_send(c), sibling_send(c)):
             copy.wait_send()
         forward(c).wait_send()
         for side in (0, 1):

time: 49.2 us -> 48.3 us (0.982)
  Pallas kernels: 47.7 us -> 46.9 us
    pallas_call x1, Pallas kernels: 47.7 us -> 46.9 us  [body(): pl.pallas_call(functools.partial(kernel, n_lat, n_lon), out_shape=jax.Sha...]
where the time goes in v6:
time: 48.3 us; the launch traced here: 48.2 us
  Pallas kernels  46.9 us (97%)
  local copies, waits for them, and re-layouts  1.32 us (3%)
    pallas_call x1, Pallas kernels, body(): pl.pallas_call(functools.partial(kernel, n_lat, n_lon), out_shape=jax.Sha...  46.9 us
    unnamed x1, local copies, waits for them, and re-layouts  1.32 us

profile of v6, /device:TPU:0, one launch (start us, length us, event | category | flops | bytes accessed | tf_op | source)
XLA Modules:
  0.0 48.2 jit_solution(17908890221814890148)
XLA Ops:
  0.0 46.9 %remap_step.1 = f32[32,64,256]{2,1,0:T(8,128)S(1)} custom-call(bf16[32,64,256]{2,1,0:T(8,128)(2,1)} %conc.1, s32[4,32]{1,0:T(4,128)} %bitcast.11, s32[4,32]{1,0:T(4,128)} %bitcast.12, f32[4,32]{1,0:T(4,128)} %bitcast.13, s32[1,32]{1,0:T(1,128)} %count_h.1, s32[1,32]{1,0:T(1,128)} %bitcast.14, f32[4,32,256]{2,1,0:T(8,128)} %rates_h.1, ...), custom_call_target="tpu_custom_call" | custom-call | tf_op jit(solution)/shard_map/remap_step/pallas_call | solution.py:436
  46.9 1.3 %copy.12 = f32[32,64,256]{2,1,0:T(8,128)} copy(f32[32,64,256]{2,1,0:T(8,128)S(1)} %remap_step.1) | data formatting | bytes 4194304
